TPU v7x, 32 devices: a whole 2x2x4 slice. The times are simulated.
32 devices in a mesh: dp: 2 (over y), head: 4 (over z), tensor: 4 (over x, core).
Axes of the slice: x: 2, y: 2, z: 4, core: 2. Of those that a mesh axis runs over, the one named last changes fastest.
Arguments:
- tokens: bfloat16 [512, 8192], P('dp', 'tensor'), may hold values from -6 to 6
- cotangent: bfloat16 [512, 8192], P('dp', 'tensor'), may hold values from -6 to 6
- w_gate: bfloat16 [8192, 29568], P('tensor', 'head'), may hold values from -0.0625 to 0.0625
- w_up: bfloat16 [8192, 29568], P('tensor', 'head'), may hold values from -0.0625 to 0.0625
- w_down: bfloat16 [29568, 8192], P('head', 'tensor'), may hold values from -0.03125 to 0.03125
- common_down_factor: bfloat16 [8192, 64], P('tensor'), may hold values from -0.0625 to 0.0625
- head_up: bfloat16 [64, 64, 8192], P('head', None, 'tensor'), may hold values from -0.0625 to 0.0625
- routes: int32 [512, 1], P('dp'), may hold values from 0 to 63
Outputs:
- grad_x: bfloat16 [512, 8192], P(('dp', 'head'), 'tensor')
- grad_shared: float32 [8192, 64], P('tensor')
- up_head_gradients: float32 [64, 64, 8192], P('head', None, 'tensor')
Inputs may be any that keep to these rules, and one draw needn't show every extreme that they name: `routes`: each token names one adapter head; the loads are skewed.
All inputs are finite; a program needn't handle non-finite values.
Results may differ from a plain program's by a relative error of at most 0.015.
Values may be sent and summed in bfloat16 or wider, within the bound.
No kernel may reach another device: no remote copies, remote signals or barrier semaphores. Data moves between devices by JAX's collectives and lax.ppermute only.
A program may use at most 256 MiB of HBM per device.

v0:
```python
import jax
import jax.numpy as jnp
from jax import lax
from jax.experimental import pallas as pl
from jax.experimental.pallas import tpu as pltpu
from jax.sharding import PartitionSpec as P


ADAPTER_SCALE = 2.0
SHARES = (5, 6, 8, 6, 4)
UNIT = 256
F32, BF16 = jnp.float32, jnp.bfloat16
ANY = pl.BlockSpec(memory_space=pl.ANY)


def contract_last(left, right):
    return lax.dot_general(
        left, right, (((1,), (1,)), ((), ())), preferred_element_type=F32
    )


def contract_first(left, right):
    return lax.dot_general(
        left, right, (((0,), (0,)), ((), ())), preferred_element_type=F32
    )


def chunk_units(hidden):
    units = pl.cdiv(hidden, UNIT)
    total, spans, left, seen = sum(SHARES), [], units, 0
    for share in SHARES:
        seen += share
        first = units - units * seen // total
        if first < left:
            spans.append((first, left - first))
        left = min(left, first)
    return spans


def step_units(span, most):
    first, count = span
    step = most
    while first % step or count % step:
        step //= 2
    return step


def params(limit_mib=48):
    return pltpu.CompilerParams(
        dimension_semantics=("arbitrary",), vmem_limit_bytes=limit_mib * 2**20
    )


def tile_copies(hidden, span, width, weights, buffers, sems):
    first, count = span
    steps = count * UNIT // width
    valid = min(hidden - (first + count) * UNIT + width, width)

    def act(k, step, use):
        def run(units):
            start = pl.multiple_of(first * UNIT + step * width, UNIT)
            use(
                pltpu.make_async_copy(
                    weights[k].at[pl.ds(start, units)],
                    buffers.at[k, step % 2, pl.ds(0, units)],
                    sems.at[k, step % 2],
                )
            )

        if valid == width:
            run(width)
        else:
            pl.when(step < steps - 1)(lambda: run(width))
            pl.when(step == steps - 1)(lambda: run(valid))

    def start(k, step):
        act(k, step, lambda copy: copy.start())

    def wait(k, step):
        act(k, step, lambda copy: copy.wait())

    return start, wait, valid


def keep_valid(value, axis, width, valid, is_last):
    if valid == width:
        return value
    unit = lax.broadcasted_iota(jnp.int32, value.shape, axis)
    return jnp.where(unit < jnp.where(is_last, valid, width), value, jnp.zeros_like(value))


def partial_sums(places, tokens, cotangent, w_gate, w_up, w_down, span, after, extra=None):
    _, count = span
    rows, d_cols = tokens.shape
    hidden = w_gate.shape[0]
    half, n = rows // 2, places.shape[0]
    block = rows // n
    width = step_units(span, 2) * UNIT
    steps = count * UNIT // width
    more = 0 if extra is None else extra.shape[1]

    def kernel(places, *refs):
        sides, weights, refs = refs[:2], refs[2:5], refs[5:]
        kept, sent, held, buffers, row_sems, sems = refs[-6:]
        step = pl.program_id(0)
        start, wait, valid = tile_copies(hidden, span, width, weights, buffers, sems)

        def row_copy(side, k):
            origin = pl.multiple_of(places[k] * block, block)
            return pltpu.make_async_copy(
                sides[side].at[pl.ds(origin, block)],
                held.at[side, pl.ds(k * block, block)],
                row_sems.at[side, k],
            )

        @pl.when(step == 0)
        def _():
            start(0, 0)
            for k in range(n):
                row_copy(0, k).start()
            start(1, 0)
            for k in range(n):
                row_copy(1, k).start()
            start(2, 0)
            for k in range(n):
                row_copy(0, k).wait()

        @pl.when(step < steps)
        def _():
            for k in range(3):
                pl.when(step + 1 < steps)(lambda: start(k, step + 1))
                if k == 2:

                    @pl.when(step == 0)
                    def _():
                        for b in range(n):
                            row_copy(1, b).wait()

                wait(k, step)
                part = contract_last(held[k // 2], buffers[k, step % 2])
                part = keep_valid(part, 1, width, valid, step == steps - 1)
                kept[k] = part[:half].astype(BF16)
                sent[k] = part[half:].astype(BF16)

        if more:

            @pl.when(step == steps)
            def _():
                for k in range(3):
                    value = refs[0][...] if k == 0 else jnp.zeros((rows, more), BF16)
                    kept[k, :, :more] = value[:half]
                    sent[k, :, :more] = value[half:]

    out = pl.BlockSpec((3, half, width), lambda j, places: (0, 0, j))
    shape = jax.ShapeDtypeStruct((3, half, count * UNIT + more), BF16)
    work = rows * d_cols * count * UNIT
    extras = [] if extra is None else [extra]
    return pl.pallas_call(
        kernel,
        grid_spec=pltpu.PrefetchScalarGridSpec(
            num_scalar_prefetch=1,
            grid=(steps + (more > 0),),
            in_specs=[ANY] * 5
            + [pl.BlockSpec(e.shape, lambda j, places: (0, 0)) for e in extras]
            + [ANY] * len(after),
            out_specs=[out, out],
            scratch_shapes=[
                pltpu.VMEM((2, rows, d_cols), BF16),
                pltpu.VMEM((3, 2, width, d_cols), BF16),
                pltpu.SemaphoreType.DMA((2, n)),
                pltpu.SemaphoreType.DMA((3, 2)),
            ],
        ),
        out_shape=[shape, shape],
        compiler_params=params(),
        cost_estimate=pl.CostEstimate(
            flops=6 * work, bytes_accessed=6 * d_cols * count * UNIT, transcendentals=0
        ),
        name="partial_sums",
    )(places, tokens, cotangent, w_gate, w_up, w_down, *extras, *after)


def pair_sum(kept, received, b, block, after):
    width = kept.shape[2]

    def kernel(mine, other, *rest):
        rest[-1][...] = (mine[...].astype(F32) + other[...].astype(F32)).astype(BF16)

    spec = pl.BlockSpec((3, block, width), lambda j: (0, b, 0))
    return pl.pallas_call(
        kernel,
        grid=(1,),
        in_specs=[spec, spec] + [ANY] * len(after),
        out_specs=pl.BlockSpec((3, block, width), lambda j: (0, 0, 0)),
        out_shape=jax.ShapeDtypeStruct((3, block, width), BF16),
        compiler_params=params(),
        cost_estimate=pl.CostEstimate(
            flops=3 * block * width, bytes_accessed=18 * block * width, transcendentals=0
        ),
        name="pair_sum",
    )(kept, received, *after)


def hidden_gradients(kept, received, others, width, block, after, extra=None):
    full = kept.shape[2]
    more = 0 if extra is None else extra.shape[1]

    def kernel(mine, other, *rest):
        rest, outs = rest[:-outputs], rest[-outputs:]

        def total(k, columns):
            value = mine[k, :, columns].astype(F32) + other[k, :, columns].astype(F32)
            for ref in rest[: len(others)]:
                value = value + ref[k, :, columns].astype(F32)
            return value

        for start in range(0, width, UNIT):
            columns = slice(start, start + UNIT)
            gate_pre, up_pre, back = (total(k, columns) for k in range(3))
            sig = jax.nn.sigmoid(gate_pre)
            scaled = back * sig
            grad = scaled * up_pre * (1.0 + gate_pre * (1.0 - sig))
            outs[0][0, :, columns] = grad.astype(BF16)
            outs[0][1, :, columns] = (scaled * gate_pre).astype(BF16)
        if full > width:
            outs[1][...] = total(0, slice(width, full)).astype(BF16)
        if more:
            outs[0][0, :, width:] = rest[len(others)][...]
            outs[0][1, :, width:] = jnp.zeros((block, more), BF16)

    outputs = 1 + (full > width)
    spec = pl.BlockSpec((3, block, full), lambda j: (0, 0, 0))
    small = pl.BlockSpec((block, max(full - width, more)), lambda j: (0, 0))
    extras = [] if extra is None else [extra]
    out = pl.pallas_call(
        kernel,
        grid=(1,),
        in_specs=[spec] * (2 + len(others)) + [small] * len(extras) + [ANY] * len(after),
        out_specs=[pl.BlockSpec((2, block, width + more), lambda j: (0, 0, 0)), small][:outputs],
        out_shape=[
            jax.ShapeDtypeStruct((2, block, width + more), BF16),
            jax.ShapeDtypeStruct((block, full - width), BF16),
        ][:outputs],
        compiler_params=params(),
        cost_estimate=pl.CostEstimate(
            flops=20 * block * width, bytes_accessed=22 * block * width,
            transcendentals=block * width,
        ),
        name="hidden_gradients",
    )(kept, received, *others, *extras, *after)
    return out if outputs > 1 else out[0]


def products(parts, w_gate, w_up, total, span, after, places=None, codes=None, factor=None):
    _, count = span
    hidden, d_cols = w_gate.shape
    block = parts[0].shape[1]
    n = len(parts)
    rows = block * n
    width = step_units(span, min(4, max(count // 2, 1))) * UNIT
    steps = count * UNIT // width
    before = [] if total is None else [total]
    extras = [] if codes is None else [codes, factor]
    picks = 0 if places is None else places.shape[0]

    def kernel(*refs):
        if picks:
            places, refs = refs[0], refs[1:]
        grads, weights, refs = refs[:n], refs[n : n + 2], refs[n + 2 :]
        if picks:
            outs, value_ref, buffers, sems = refs[-3 - picks : -3], *refs[-3:]
        else:
            value_ref, buffers, sems = refs[-3:]
        step = pl.program_id(0)
        start, wait, valid = tile_copies(hidden, span, width, weights, buffers, sems)

        @pl.when(step == 0)
        def _():
            start(0, 0)
            start(1, 0)
            value_ref[...] = refs[0][...] if before else jnp.zeros_like(value_ref)

        pl.when(step + 1 < steps)(lambda: start(0, step + 1))
        wait(0, step)
        value = value_ref[...]
        for k in range(2):
            if k == 1:
                pl.when(step + 1 < steps)(lambda: start(1, step + 1))
                wait(1, step)
            tile = keep_valid(buffers[k, step % 2], 0, width, valid, step == steps - 1)
            left = jnp.concatenate([g[k] for g in grads], axis=0)
            value = value + jnp.dot(left, tile, preferred_element_type=F32)
        value_ref[...] = value

        if extras:

            @pl.when(step == 0)
            def _():
                code, rest = refs[len(before) : len(before) + 2]
                value_ref[...] += jnp.dot(code[...], rest[...], preferred_element_type=F32)

        if picks:

            @pl.when(step == steps - 1)
            def _():
                for k, out in enumerate(outs):
                    begin = pl.multiple_of(places[k] * block, block)
                    out[...] = value_ref[pl.ds(begin, block)].astype(out.dtype)

    grad = pl.BlockSpec((2, block, width), lambda j, *_: (0, 0, j))
    whole = pl.BlockSpec((rows, d_cols), lambda j, *_: (0, 0))
    piece = pl.BlockSpec((block, d_cols), lambda j, *_: (0, 0))
    work = rows * d_cols * count * UNIT
    in_specs = [grad] * n + [ANY, ANY] + [whole] * len(before)
    in_specs += [pl.BlockSpec(e.shape, lambda j, *_: (0, 0)) for e in extras]
    scratch = [
        pltpu.VMEM((2, 2, width, d_cols), BF16),
        pltpu.SemaphoreType.DMA((2, 2)),
    ]
    if picks:
        out_specs = [piece] * picks
        out_shape = [
            jax.ShapeDtypeStruct((block, d_cols), BF16 if k else F32) for k in range(picks)
        ]
        scratch = [pltpu.VMEM((rows, d_cols), F32)] + scratch
    else:
        out_specs = whole
        out_shape = jax.ShapeDtypeStruct((rows, d_cols), F32)
    return pl.pallas_call(
        kernel,
        grid_spec=pltpu.PrefetchScalarGridSpec(
            num_scalar_prefetch=1 if picks else 0,
            grid=(steps,),
            in_specs=in_specs + [ANY] * len(after),
            out_specs=out_specs,
            scratch_shapes=scratch,
        ),
        out_shape=out_shape,
        compiler_params=params(),
        cost_estimate=pl.CostEstimate(
            flops=4 * work, bytes_accessed=4 * d_cols * count * UNIT, transcendentals=0
        ),
        name="products",
    )(*([places] if picks else []), *parts, w_gate, w_up, *before, *extras, *after)


def ordered(value, *earlier):
    return lax.optimization_barrier((value, *earlier))[0]


def backward(tokens, cotangent, w_gate, w_up, w_down, common_down_factor, head_up, routes):
    tok_rows, d_cols = tokens.shape
    hidden = w_gate.shape[1]
    rank = common_down_factor.shape[1]
    local_heads = head_up.shape[0]
    n_tensor, n_head, n_dp = (lax.axis_size(a) for a in ("tensor", "head", "dp"))
    chips = n_tensor // 2
    me = lax.axis_index("tensor")
    my_chip, my_core = me // 2, me % 2
    my_head, my_dp = lax.axis_index("head"), lax.axis_index("dp")
    block = tok_rows // n_tensor
    out_rows = tok_rows // n_head
    if out_rows != block or n_tensor % 2:
        raise ValueError("unsupported mesh")

    def place_of(owner):
        core, chip = owner // chips, owner % chips
        return (core + my_core) % 2 * chips + (chip - my_chip) % chips

    order = jnp.arange(n_tensor, dtype=jnp.int32)
    places = (order // chips + my_core) % 2 * chips + (order % chips + my_chip) % chips

    def relative(rows):
        return jnp.concatenate(
            [
                lax.dynamic_slice_in_dim(rows, places[k] * block, block, 0)
                for k in range(n_tensor)
            ],
            axis=0,
        )

    def absolute(rows):
        return jnp.concatenate(
            [
                lax.dynamic_slice_in_dim(rows, place_of(k) * block, block, 0)
                for k in range(n_tensor)
            ],
            axis=0,
        )

    def swap_core(value):
        return lax.ppermute(value, "tensor", [(i, i ^ 1) for i in range(n_tensor)])

    def shift_chip(value, step):
        pairs = [(i, (i // 2 + step) % chips * 2 + i % 2) for i in range(n_tensor)]
        return lax.ppermute(value, "tensor", pairs)

    def shift(value, axis, count, step):
        return lax.ppermute(value, axis, [(i, (i + step) % count) for i in range(count)])

    head_ids = my_head * local_heads + jnp.arange(local_heads, dtype=jnp.int32)[None, :]

    def adapter_parts(earlier):
        own_tokens, own_cotangent = ordered(tokens, earlier), ordered(cotangent, earlier)
        codes = jnp.dot(own_tokens, common_down_factor, preferred_element_type=F32)
        separated = contract_last(
            own_cotangent, head_up.reshape(local_heads * rank, d_cols)
        )
        code_grad = ADAPTER_SCALE * jnp.sum(
            separated.reshape(tok_rows, local_heads, rank)
            * (routes == head_ids).astype(F32)[:, :, None],
            axis=1,
        )
        return relative(jnp.concatenate([codes, code_grad], axis=1).astype(BF16))

    spans = chunk_units(hidden)
    count = len(spans)
    w_gate, w_up = w_gate.T, w_up.T
    sums, grads, after = [], [], []
    adapter = {}

    def finish(c, after):
        kept, received, others = sums[c]
        own = hidden_gradients(
            kept, received, others, spans[c][1] * UNIT, block, after,
            adapter["own"] if c == 3 else None,
        )
        if c == 1:
            own, adapter["own"] = own
        near = swap_core(own)
        far = [shift_chip(own, -b) for b in range(1, chips)]
        grads.append([own] + far + [near] + [swap_core(f) for f in far])
        return own

    other_cotangents = [shift(cotangent, "dp", n_dp, s) for s in range(1, n_dp)]

    for c, span in enumerate(spans):
        kept, sent = partial_sums(
            places, tokens, cotangent, w_gate, w_up, w_down, span, after,
            adapter["part"] if c == 1 else None,
        )
        received = swap_core(sent)
        after = [kept]
        if c == 0:
            adapter["part"] = adapter_parts(kept)
            after = [adapter["part"]]
        if c >= 2:
            after = [finish(c - 2, after)]
        pairs = [pair_sum(kept, received, b, block, after) for b in range(1, chips)]
        others = [shift_chip(p, b + 1) for b, p in enumerate(pairs)]
        sums.append((kept, received, others))
        after = pairs[-1:]

    rows = None
    head_places = place_of((my_head + jnp.arange(n_head, dtype=jnp.int32)) % n_head)
    for c, span in enumerate(spans):
        extra = {}
        if c == 3:
            start = span[1] * UNIT
            adapter["all"] = jnp.concatenate([g[0, :, start:] for g in grads[c]], axis=0)
            extra = dict(codes=adapter["all"][:, rank:], factor=common_down_factor.T)
        rows = products(
            grads[c], w_gate, w_up, rows, span, after,
            head_places if c == count - 1 else None, **extra,
        )
        if c == count - 1:
            break
        after = [rows]
        if len(grads) < count:
            after = [finish(len(grads), after)]
        if c == 3:
            both = absolute(ordered(adapter["all"], rows))
            codes = jnp.concatenate([both[:, :rank], routes.astype(BF16)], axis=1)
            other_codes = [shift(codes, "dp", n_dp, s) for s in range(1, n_dp)]
            part = both[:, rank:]
            head_parts = [shift(part, "head", n_head, s) for s in range(1, n_head)]
            after = after + [codes, part]

    def by_group(own, others):
        doubled = jnp.concatenate([own] + others[::-1], axis=0)
        doubled = jnp.concatenate([doubled, doubled], axis=0)
        count = own.shape[0]
        start = (n_dp - my_dp) % n_dp * count
        return lax.dynamic_slice_in_dim(doubled, start, n_dp * count, 0)

    received = [shift(rows[s], "head", n_head, s) for s in range(1, n_head)]

    code_grad = ordered(part, rows[0]).astype(F32)
    for other in head_parts:
        code_grad = code_grad + other.astype(F32)
    code_grad = code_grad.astype(BF16)
    shared = contract_first(code_grad, tokens)
    grad_shared = shared
    for s in range(1, n_dp):
        grad_shared = grad_shared + shift(shared, "dp", n_dp, s)
    grad_shared = grad_shared.T

    all_codes = by_group(ordered(codes, rows[0], shared), other_codes)
    all_cotangents = by_group(ordered(cotangent, rows[0], shared), other_cotangents)
    masked = jnp.where(
        (all_codes[:, rank:].astype(jnp.int32) == head_ids)[:, :, None],
        all_codes[:, None, :rank],
        jnp.zeros((), BF16),
    ).reshape(n_dp * tok_rows, local_heads * rank)
    up_heads = ADAPTER_SCALE * contract_first(masked, all_cotangents)
    up_heads = up_heads.reshape(local_heads, rank, d_cols)

    grad_x = rows[0]
    for other in received:
        grad_x = grad_x + other.astype(F32)
    return grad_x.astype(BF16), grad_shared, up_heads


def solution(mesh):
    placed = (
        P("dp", "tensor"),
        P("dp", "tensor"),
        P("tensor", "head"),
        P("tensor", "head"),
        P("head", "tensor"),
        P("tensor", None),
        P("head", None, "tensor"),
        P("dp", None),
    )
    return jax.shard_map(
        backward,
        mesh=mesh,
        in_specs=placed,
        out_specs=(P(("dp", "head"), "tensor"), P("tensor", None), P("head", None, "tensor")),
        check_vma=False,
    )
```

profile of v0, /device:TPU:0, one launch (start us, length us, event | category | flops | bytes accessed | tf_op | source)
XLA Modules:
  0.0 229.5 jit_solution(174811297364084207)
XLA Ops:
  0.7 1.2 copy-done
  1.9 1.2 copy-done.2
  3.1 12.6 %partial_sums.5 = (bf16[3,128,1280]{2,1,0:T(8,128)(2,1)S(1)}, bf16[3,128,1280]{2,1,0:T(8,128)(2,1)}) custom-call(s32[4]{0:T(128)S(1)} %fusion.17.places, bf16[256,2048]{1,0:T(8,128)(2,1)S(1)} %copy-done, bf16[256,2048]{1,0:T(8,128)(2,1)S(1)} %copy-done.2, bf16[7392,2048]{1,0:T(8,128)(2,1)} %bitcast.30, bf16[7392,2048]{1,0:T(8,128)(2,1)} %bitcast.40, ...), custom_call_target="tpu_custom_call" | custom-call | flops 4026531840 | bytes 15728640 | tf_op jit(solution)/shard_map/partial_sums/pallas_call | solution.py:158
  15.7 0.6 collective-permute-start
  16.3 0.4 convolution_convert_fusion
  16.8 0.6 fusion.29
  20.2 3.5 %fusion.4 = f32[256,64]{0,1:T(8,128)S(1)} fusion(bf16[16,64,2048]{2,1,0:T(8,128)(2,1)} %param.14, bf16[256,2048]{1,0:T(8,128)(2,1)S(1)} %copy-done.3, f32[256,16]{0,1:T(8,128)S(1)} %compare_convert_fusion), kind=kOutput, calls=%fused_computation.9 | convolution fusion | flops 1074249728 | bytes 5324800 | tf_op jit(solution)/shard_map/dot_general | solution.py:17
  24.0 1.2 pair_sum.5.refs_6_
  25.2 9.5 %partial_sums.6 = (bf16[3,128,1664]{2,1,0:T(8,128)(2,1)S(1)}, bf16[3,128,1664]{2,1,0:T(8,128)(2,1)S(1)}) custom-call(s32[4]{0:T(128)S(1)} %fusion.17.places, bf16[256,2048]{1,0:T(8,128)(2,1)S(1)} %copy-done.1, bf16[256,2048]{1,0:T(8,128)(2,1)S(1)} %copy-done.3, bf16[7392,2048]{1,0:T(8,128)(2,1)} %bitcast.31, bf16[7392,2048]{1,0:T(8,128)(2,1)} %bitcast.41, ...), custom_call_target="tpu_custom_call" | custom-call | flops 4831838208 | bytes 18874368 | tf_op jit(solution)/shard_map/partial_sums/pallas_call | solution.py:158
  34.8 2.9 %collective-permute-done.1.other = bf16[3,128,1664]{2,1,0:T(8,128)(2,1)S(1)} collective-permute-done((bf16[3,128,1664]{2,1,0:T(8,128)(2,1)S(1)}, bf16[3,128,1664]{2,1,0:T(8,128)(2,1)S(1)}, u32[]{:S(2)}, u32[]{:S(2)}) %collective-permute-start.1) | collective-permute-done | bytes 1277984 | tf_op jit(solution)/shard_map/ppermute | solution.py:392
  37.7 0.4 pair_sum.6.refs_5_
  38.1 11.5 %partial_sums.7 = (bf16[3,128,2048]{2,1,0:T(8,128)(2,1)S(1)}, bf16[3,128,2048]{2,1,0:T(8,128)(2,1)S(1)}) custom-call(s32[4]{0:T(128)S(1)} %fusion.17.places, bf16[256,2048]{1,0:T(8,128)(2,1)S(1)} %copy-done.1, bf16[256,2048]{1,0:T(8,128)(2,1)S(1)} %copy-done.3, bf16[7392,2048]{1,0:T(8,128)(2,1)} %bitcast.32, bf16[7392,2048]{1,0:T(8,128)(2,1)} %bitcast.42, ...), custom_call_target="tpu_custom_call" | custom-call | flops 6442450944 | bytes 25165824 | tf_op jit(solution)/shard_map/partial_sums/pallas_call | solution.py:158
  49.8 2.8 %collective-permute-start.3 = (bf16[3,64,1280]{2,1,0:T(8,128)(2,1)S(1)}, bf16[3,64,1280]{2,1,0:T(8,128)(2,1)S(1)}, u32[]{:S(2)}, u32[]{:S(2)}) collective-permute-start(bf16[3,64,1280]{2,1,0:T(8,128)(2,1)S(1)} %pair_sum.5.refs_6_), channel_id=1, source_target_pairs={{0,2},{1,3},{2,0},{3,1},{4,6},{5,7},{6,4},{7,5},{8,10},{9,11},{10,... | collective-permute-start | bytes 1474568 | tf_op jit(solution)/shard_map/ppermute | solution.py:396
  52.6 11.5 %collective-permute-done.3.rest_0_ = bf16[3,64,1280]{2,1,0:T(8,128)(2,1)S(1)} collective-permute-done((bf16[3,64,1280]{2,1,0:T(8,128)(2,1)S(1)}, bf16[3,64,1280]{2,1,0:T(8,128)(2,1)S(1)}, u32[]{:S(2)}, u32[]{:S(2)}) %collective-permute-start.3) | collective-permute-done | bytes 491552 | tf_op jit(solution)/shard_map/ppermute | solution.py:396
  64.1 1.3 hidden_gradients.5.rest_0_.refs_0_
  65.7 9.2 %partial_sums.8 = (bf16[3,128,1536]{2,1,0:T(8,128)(2,1)S(1)}, bf16[3,128,1536]{2,1,0:T(8,128)(2,1)S(1)}) custom-call(s32[4]{0:T(128)S(1)} %fusion.17.places, bf16[256,2048]{1,0:T(8,128)(2,1)S(1)} %copy-done.1, bf16[256,2048]{1,0:T(8,128)(2,1)S(1)} %copy-done.3, bf16[7392,2048]{1,0:T(8,128)(2,1)} %bitcast.33, bf16[7392,2048]{1,0:T(8,128)(2,1)} %bitcast.43, ...), custom_call_target="tpu_custom_call" | custom-call | flops 4831838208 | bytes 18874368 | tf_op jit(solution)/shard_map/partial_sums/pallas_call | solution.py:158
  74.9 1.8 collective-permute-start.5
  76.7 0.3 collective-permute-start.7
  77.0 15.2 %collective-permute-done.5.rest_0_ = bf16[3,64,1664]{2,1,0:T(8,128)(2,1)S(1)} collective-permute-done((bf16[3,64,1664]{2,1,0:T(8,128)(2,1)S(1)}, bf16[3,64,1664]{2,1,0:T(8,128)(2,1)S(1)}, u32[]{:S(2)}, u32[]{:S(2)}) %collective-permute-start.5) | collective-permute-done | bytes 639008 | tf_op jit(solution)/shard_map/ppermute | solution.py:396
  92.2 1.2 hidden_gradients.6
  93.4 1.0 pair_sum.8.refs_5_
  94.4 1.0 copy-done.8
  95.4 7.1 %partial_sums.9 = (bf16[3,128,1024]{2,1,0:T(8,128)(2,1)S(1)}, bf16[3,128,1024]{2,1,0:T(8,128)(2,1)S(1)}) custom-call(s32[4]{0:T(128)S(1)} %fusion.17.places, bf16[256,2048]{1,0:T(8,128)(2,1)S(1)} %copy-done.1, bf16[256,2048]{1,0:T(8,128)(2,1)S(1)} %copy-done.3, bf16[7392,2048]{1,0:T(8,128)(2,1)} %bitcast.34, bf16[7392,2048]{1,0:T(8,128)(2,1)} %bitcast.44, ...), custom_call_target="tpu_custom_call" | custom-call | flops 3221225472 | bytes 12582912 | tf_op jit(solution)/shard_map/partial_sums/pallas_call | solution.py:158
  102.5 1.8 collective-permute-start.12
  104.5 0.3 collective-permute-start.9
  104.8 11.4 %collective-permute-done.12.refs_1_ = bf16[2,64,1280]{2,1,0:T(8,128)(2,1)} collective-permute-done((bf16[2,64,1280]{2,1,0:T(8,128)(2,1)S(1)}, bf16[2,64,1280]{2,1,0:T(8,128)(2,1)}, u32[]{:S(2)}, u32[]{:S(2)}) %collective-permute-start.12) | collective-permute-done | bytes 327712 | tf_op jit(solution)/shard_map/ppermute | solution.py:396
  116.2 1.7 collective-permute-start.15
  118.0 2.4 %hidden_gradients.7.rest_0_.refs_0_ = bf16[2,64,2048]{2,1,0:T(8,128)(2,1)} custom-call(bf16[3,128,2048]{2,1,0:T(8,128)(2,1)S(1)} %get-tuple-element.31.rest_1_.mine, bf16[3,128,2048]{2,1,0:T(8,128)(2,1)S(1)} %collective-permute-done.2.other, bf16[3,64,2048]{2,1,0:T(8,128)(2,1)} %collective-permute-done.7.rest_0_, ...), custom_call_target="tpu_custom_call" | custom-call | flops 2621440 | bytes 2883584 | tf_op jit(solution)/shard_map/hidden_gradients/pallas_call | solution.py:235
  120.4 0.7 copy-done.17
  121.2 0.3 collective-permute-start.22
  121.4 3.2 %collective-permute-done.9.refs_1_ = bf16[2,64,1536]{2,1,0:T(8,128)(2,1)} collective-permute-done((bf16[2,64,1536]{2,1,0:T(8,128)(2,1)}, bf16[2,64,1536]{2,1,0:T(8,128)(2,1)}, u32[]{:S(2)}, u32[]{:S(2)}) %collective-permute-start.9) | collective-permute-done | bytes 393248 | tf_op jit(solution)/shard_map/ppermute | solution.py:396
  124.7 0.9 copy-done.10
  125.5 0.5 collective-permute-start.11
  126.3 1.1 copy-done.6
  127.4 1.1 copy-done.11
  128.6 1.8 collective-permute-start.33
  130.5 1.0 copy-done.14
  131.5 1.0 copy-done.18
  132.4 7.7 %products.5.rest_2_.refs_6_ = f32[256,2048]{1,0:T(8,128)S(1)} custom-call(bf16[2,64,1280]{2,1,0:T(8,128)(2,1)S(1)} %copy-done.14, bf16[2,64,1280]{2,1,0:T(8,128)(2,1)} %collective-permute-done.12.refs_1_, bf16[2,64,1280]{2,1,0:T(8,128)(2,1)S(1)} %copy-done.18, bf16[2,64,1280]{2,1,0:T(8,128)(2,1)} %collective-permute-done.14.refs_3_, ...), custom_call_target="tpu_custom_call" | custom-call | flops 2684354560 | bytes 10485760 | tf_op jit(solution)/shard_map/products/pallas_call | solution.py:329
  140.2 7.8 %collective-permute-done.22.refs_1_ = bf16[2,64,2048]{2,1,0:T(8,128)(2,1)} collective-permute-done((bf16[2,64,2048]{2,1,0:T(8,128)(2,1)}, bf16[2,64,2048]{2,1,0:T(8,128)(2,1)}, u32[]{:S(2)}, u32[]{:S(2)}) %collective-permute-start.22) | collective-permute-done | bytes 524320 | tf_op jit(solution)/shard_map/ppermute | solution.py:396
  148.0 0.5 collective-permute-start.24
  148.5 1.5 hidden_gradients.8.refs_7_.refs_0_
  150.0 1.8 collective-permute-start.8
  151.8 0.3 collective-permute-start.19
  152.1 7.2 %products.6.rest_1_.refs_6_ = f32[256,2048]{1,0:T(8,128)S(1)} custom-call(bf16[2,64,1536]{2,1,0:T(8,128)(2,1)} %get-tuple-element.35.rest_0_.refs_0_, bf16[2,64,1536]{2,1,0:T(8,128)(2,1)} %collective-permute-done.9.refs_1_, bf16[2,64,1536]{2,1,0:T(8,128)(2,1)} %collective-permute-done.10.refs_2_, bf16[2,64,1536]{2,1,0:T(8,128)(2,1)} %collective-permute-done.11.refs_3_, ...), custom_call_target="tpu_custom_call" | custom-call | flops 3221225472 | bytes 12582912 | tf_op jit(solution)/shard_map/products/pallas_call | solution.py:329
  159.3 2.7 %collective-permute-done.8.rest_0_ = bf16[3,64,1024]{2,1,0:T(8,128)(2,1)S(1)} collective-permute-done((bf16[3,64,1024]{2,1,0:T(8,128)(2,1)S(1)}, bf16[3,64,1024]{2,1,0:T(8,128)(2,1)S(1)}, u32[]{:S(2)}, u32[]{:S(2)}) %collective-permute-start.8) | collective-permute-done | bytes 393248 | tf_op jit(solution)/shard_map/ppermute | solution.py:396
  162.3 1.8 collective-permute-start.16
  164.3 9.8 %products.7.refs_6_.refs_9_ = f32[256,2048]{1,0:T(8,128)S(1)} custom-call(bf16[2,64,2048]{2,1,0:T(8,128)(2,1)} %hidden_gradients.7.rest_0_.refs_0_, bf16[2,64,2048]{2,1,0:T(8,128)(2,1)} %collective-permute-done.22.refs_1_, bf16[2,64,2048]{2,1,0:T(8,128)(2,1)S(1)} %collective-permute-done.23.refs_2_, ...), custom_call_target="tpu_custom_call" | custom-call | flops 4294967296 | bytes 16777216 | tf_op jit(solution)/shard_map/products/pallas_call | solution.py:329
  174.1 0.4 collective-permute-start.21
  174.5 1.3 collective-permute-done.16.refs_2_
  176.1 8.8 %products.8.refs_7_.refs_8_ = f32[256,2048]{1,0:T(8,128)S(1)} custom-call(bf16[2,64,1664]{2,1,0:T(8,128)(2,1)S(1)} %hidden_gradients.8.refs_7_.refs_0_, bf16[2,64,1664]{2,1,0:T(8,128)(2,1)S(1)} %collective-permute-done.19.refs_1_, bf16[2,64,1664]{2,1,0:T(8,128)(2,1)S(1)} %collective-permute-done.20.refs_2_, ...), custom_call_target="tpu_custom_call" | custom-call | flops 3221225472 | bytes 12582912 | tf_op jit(solution)/shard_map/products/pallas_call | solution.py:329
  185.0 3.8 %collective-permute-start.30 = (bf16[256,64]{1,0:T(8,128)(2,1)S(1)}, bf16[256,64]{1,0:T(8,128)(2,1)S(1)}, u32[]{:S(2)}, u32[]{:S(2)}) collective-permute-start(bf16[256,64]{1,0:T(8,128)(2,1)S(1)} %get-tuple-element.44.refs_10_), channel_id=1, source_target_pairs={{0,12},{4,0},{8,4},{12,8},{1,13},{5,1},{9,5},{13,9},{2,14},{6,2},{... | collective-permute-start | bytes 98312 | tf_op jit(solution)/shard_map/ppermute | solution.py:399
  188.9 1.1 collective-permute-start.28
  190.0 1.5 collective-permute-start.32
  191.5 6.4 %products.9 = (f32[64,2048]{1,0:T(8,128)S(1)}, bf16[64,2048]{1,0:T(8,128)(2,1)S(1)}, bf16[64,2048]{1,0:T(8,128)(2,1)S(1)}, bf16[64,2048]{1,0:T(8,128)(2,1)}) custom-call(s32[4]{0:T(128)S(1)} %fusion.15.refs_0_, bf16[2,64,1024]{2,1,0:T(8,128)(2,1)S(1)} %hidden_gradients.9.refs_7_.refs_1_, bf16[2,64,1024]{2,1,0:T(8,128)(2,1)S(1)} %collective-permute-done.16.refs_2_, ...), custom_call_target="tpu_custom_call" | custom-call | flops 2147483648 | bytes 8388608 | tf_op jit(solution)/shard_map/products/pallas_call | solution.py:329
  197.9 1.1 fusion.9
  199.1 0.5 collective-permute-start.31
  199.6 2.8 %collective-permute-start.27 = (bf16[64,2048]{1,0:T(8,128)(2,1)}, bf16[64,2048]{1,0:T(8,128)(2,1)S(1)}, u32[]{:S(2)}, u32[]{:S(2)}) collective-permute-start(bf16[64,2048]{1,0:T(8,128)(2,1)} %get-tuple-element.43), channel_id=1, source_target_pairs={{0,12},{4,0},{8,4},{12,8},{1,13},{5,1},{9,5},{13,9},{2,14},{6,2},{... | collective-permute-start | bytes 786440 | tf_op jit(solution)/shard_map/ppermute | solution.py:399
  202.4 1.1 collective-permute-start.26
  203.6 0.9 fusion.8
  205.0 7.3 %convolution_multiply_fusion = f32[1024,2048]{1,0:T(8,128)} fusion(bf16[512,1024]{0,1:T(8,128)(2,1)S(1)} %bitcast.51, s32[]{:T(128)S(6)} %select_n.139, bf16[256,2048]{1,0:T(8,128)(2,1)S(1)} %copy-done.3, bf16[256,2048]{1,0:T(8,128)(2,1)} %collective-permute-done.33), kind=kOutput, calls=%fused_computation | convolution fusion | flops 2157969408 | bytes 11534340 | tf_op jit(solution)/shard_map/dot_general | solution.py:23
  212.3 13.6 %collective-permute-done.26 = bf16[64,2048]{1,0:T(8,128)(2,1)S(1)} collective-permute-done((bf16[64,2048]{1,0:T(8,128)(2,1)S(1)}, bf16[64,2048]{1,0:T(8,128)(2,1)S(1)}, u32[]{:S(2)}, u32[]{:S(2)}) %collective-permute-start.26) | collective-permute-done | bytes 262176 | tf_op jit(solution)/shard_map/ppermute | solution.py:399
  225.9 1.8 add_convert_fusion
  227.7 1.9 add_bitcast_fusion
  (101 shorter events, 3.2 us)
Async XLA Ops:
  0.7 1.2 copy-start
  1.9 1.2 copy-start.2
  3.1 13.1 %copy-start.1 = (bf16[256,2048]{1,0:T(8,128)(2,1)S(1)}, bf16[256,2048]{1,0:T(8,128)(2,1)}, u32[]{:S(2)}) copy-start(bf16[256,2048]{1,0:T(8,128)(2,1)} %refs_0_.9) | copy-start | bytes 3145732
  3.1 13.1 %copy-start.15 = (bf16[2048,64]{0,1:T(8,128)(2,1)S(1)}, bf16[2048,64]{0,1:T(8,128)(2,1)}, u32[]{:S(2)}) copy-start(bf16[2048,64]{0,1:T(8,128)(2,1)} %param.13) | copy-start | bytes 786436
  3.1 13.7 %copy-start.19 = (s32[256,1]{0,1:T(1,128)S(1)}, s32[256,1]{0,1:T(1,128)}, u32[]{:S(2)}) copy-start(s32[256,1]{0,1:T(1,128)} %param.15) | copy-start | bytes 3076
  3.1 17.1 %copy-start.3 = (bf16[256,2048]{1,0:T(8,128)(2,1)S(1)}, bf16[256,2048]{1,0:T(8,128)(2,1)}, u32[]{:S(2)}) copy-start(bf16[256,2048]{1,0:T(8,128)(2,1)} %refs_1_.9) | copy-start | bytes 3145732
  15.7 8.3 %collective-permute-start = (bf16[3,128,1280]{2,1,0:T(8,128)(2,1)}, bf16[3,128,1280]{2,1,0:T(8,128)(2,1)}, u32[]{:S(2)}, u32[]{:S(2)}) collective-permute-start(bf16[3,128,1280]{2,1,0:T(8,128)(2,1)} %get-tuple-element.28), channel_id=1, source_target_pairs={{0,1},{1,0},{2,3},{3,2},{4,5},{5,4},{6,7},{7,6},{8,9},{9,8},{10,11... | collective-permute-start | bytes 2949128 | tf_op jit(solution)/shard_map/ppermute | solution.py:392
  16.3 0.5 copy-start.20
  34.6 3.1 %collective-permute-start.1 = (bf16[3,128,1664]{2,1,0:T(8,128)(2,1)S(1)}, bf16[3,128,1664]{2,1,0:T(8,128)(2,1)S(1)}, u32[]{:S(2)}, u32[]{:S(2)}) collective-permute-start(bf16[3,128,1664]{2,1,0:T(8,128)(2,1)S(1)} %get-tuple-element.30), channel_id=1, source_target_pairs={{0,1},{1,0},{2,3},{3,2},{4,5},{5,4},{6,7},{7,6},{8,9},{9,8},{10,11... | collective-permute-start | bytes 3833864 | tf_op jit(solution)/shard_map/ppermute | solution.py:392
  49.6 15.9 %collective-permute-start.2 = (bf16[3,128,2048]{2,1,0:T(8,128)(2,1)S(1)}, bf16[3,128,2048]{2,1,0:T(8,128)(2,1)S(1)}, u32[]{:S(2)}, u32[]{:S(2)}) collective-permute-start(bf16[3,128,2048]{2,1,0:T(8,128)(2,1)S(1)} %get-tuple-element.32), channel_id=1, source_target_pairs={{0,1},{1,0},{2,3},{3,2},{4,5},{5,4},{6,7},{7,6},{8,9},{9,8},{10,11... | collective-permute-start | bytes 4718600 | tf_op jit(solution)/shard_map/ppermute | solution.py:392
  49.8 14.4 %collective-permute-start.3 = (bf16[3,64,1280]{2,1,0:T(8,128)(2,1)S(1)}, bf16[3,64,1280]{2,1,0:T(8,128)(2,1)S(1)}, u32[]{:S(2)}, u32[]{:S(2)}) collective-permute-start(bf16[3,64,1280]{2,1,0:T(8,128)(2,1)S(1)} %pair_sum.5.refs_6_), channel_id=1, source_target_pairs={{0,2},{1,3},{2,0},{3,1},{4,6},{5,7},{6,4},{7,5},{8,10},{9,11},{10,... | collective-permute-start | bytes 1474568 | tf_op jit(solution)/shard_map/ppermute | solution.py:396
  65.5 38.9 %copy-start.13 = (bf16[2,64,1280]{2,1,0:T(8,128)(2,1)}, bf16[2,64,1280]{2,1,0:T(8,128)(2,1)S(1)}, u32[]{:S(2)}) copy-start(bf16[2,64,1280]{2,1,0:T(8,128)(2,1)S(1)} %hidden_gradients.5.rest_0_.refs_0_) | copy-start | bytes 983044
  74.8 18.6 %collective-permute-start.4 = (bf16[3,128,1536]{2,1,0:T(8,128)(2,1)S(1)}, bf16[3,128,1536]{2,1,0:T(8,128)(2,1)S(1)}, u32[]{:S(2)}, u32[]{:S(2)}) collective-permute-start(bf16[3,128,1536]{2,1,0:T(8,128)(2,1)S(1)} %get-tuple-element.34), channel_id=1, source_target_pairs={{0,1},{1,0},{2,3},{3,2},{4,5},{5,4},{6,7},{7,6},{8,9},{9,8},{10,11... | collective-permute-start | bytes 3538952 | tf_op jit(solution)/shard_map/ppermute | solution.py:392
  74.9 17.3 %collective-permute-start.5 = (bf16[3,64,1664]{2,1,0:T(8,128)(2,1)S(1)}, bf16[3,64,1664]{2,1,0:T(8,128)(2,1)S(1)}, u32[]{:S(2)}, u32[]{:S(2)}) collective-permute-start(bf16[3,64,1664]{2,1,0:T(8,128)(2,1)S(1)} %pair_sum.6.refs_5_), channel_id=1, source_target_pairs={{0,2},{1,3},{2,0},{3,1},{4,6},{5,7},{6,4},{7,5},{8,10},{9,11},{10,... | collective-permute-start | bytes 1916936 | tf_op jit(solution)/shard_map/ppermute | solution.py:396
  76.7 41.2 %collective-permute-start.7 = (bf16[3,64,2048]{2,1,0:T(8,128)(2,1)S(1)}, bf16[3,64,2048]{2,1,0:T(8,128)(2,1)}, u32[]{:S(2)}, u32[]{:S(2)}) collective-permute-start(bf16[3,64,2048]{2,1,0:T(8,128)(2,1)S(1)} %pair_sum.7.refs_5_), channel_id=1, source_target_pairs={{0,2},{1,3},{2,0},{3,1},{4,6},{5,7},{6,4},{7,5},{8,10},{9,11},{10,... | collective-permute-start | bytes 2359304 | tf_op jit(solution)/shard_map/ppermute | solution.py:396
  94.4 1.0 copy-start.8
  102.4 18.0 %copy-start.5 = (bf16[3,128,1024]{2,1,0:T(8,128)(2,1)}, bf16[3,128,1024]{2,1,0:T(8,128)(2,1)S(1)}, u32[]{:S(2)}) copy-start(bf16[3,128,1024]{2,1,0:T(8,128)(2,1)S(1)} %get-tuple-element.36.rest_1_.mine) | copy-start | bytes 2359300
  102.5 22.2 %collective-permute-start.6 = (bf16[3,128,1024]{2,1,0:T(8,128)(2,1)S(1)}, bf16[3,128,1024]{2,1,0:T(8,128)(2,1)S(1)}, u32[]{:S(2)}, u32[]{:S(2)}) collective-permute-start(bf16[3,128,1024]{2,1,0:T(8,128)(2,1)S(1)} %get-tuple-element.37), channel_id=1, source_target_pairs={{0,1},{1,0},{2,3},{3,2},{4,5},{5,4},{6,7},{7,6},{8,9},{9,8},{10,11... | collective-permute-start | bytes 2359304 | tf_op jit(solution)/shard_map/ppermute | solution.py:392
  102.5 13.7 %collective-permute-start.12 = (bf16[2,64,1280]{2,1,0:T(8,128)(2,1)S(1)}, bf16[2,64,1280]{2,1,0:T(8,128)(2,1)}, u32[]{:S(2)}, u32[]{:S(2)}) collective-permute-start(bf16[2,64,1280]{2,1,0:T(8,128)(2,1)S(1)} %hidden_gradients.5.rest_0_.refs_0_), channel_id=1, source_target_pairs={{0,2},{1,3},{2,0},{3,1},{4,6},{5,7},{6,4},{7,5},{8,10},{9,11},{10,... | collective-permute-start | bytes 983048 | tf_op jit(solution)/shard_map/ppermute | solution.py:396
  104.3 16.1 %collective-permute-start.13 = (bf16[2,64,1280]{2,1,0:T(8,128)(2,1)S(1)}, bf16[2,64,1280]{2,1,0:T(8,128)(2,1)S(1)}, u32[]{:S(2)}, u32[]{:S(2)}) collective-permute-start(bf16[2,64,1280]{2,1,0:T(8,128)(2,1)S(1)} %hidden_gradients.5.rest_0_.refs_0_), channel_id=1, source_target_pairs={{0,1},{1,0},{2,3},{3,2},{4,5},{5,4},{6,7},{7,6},{8,9},{9,8},{10,11... | collective-permute-start | bytes 983048 | tf_op jit(solution)/shard_map/ppermute | solution.py:392
  104.5 20.2 %collective-permute-start.9 = (bf16[2,64,1536]{2,1,0:T(8,128)(2,1)}, bf16[2,64,1536]{2,1,0:T(8,128)(2,1)}, u32[]{:S(2)}, u32[]{:S(2)}) collective-permute-start(bf16[2,64,1536]{2,1,0:T(8,128)(2,1)} %get-tuple-element.35.rest_0_.refs_0_), channel_id=1, source_target_pairs={{0,2},{1,3},{2,0},{3,1},{4,6},{5,7},{6,4},{7,5},{8,10},{9,11},{10,... | collective-permute-start | bytes 1179656 | tf_op jit(solution)/shard_map/ppermute | solution.py:396
  116.2 31.8 %collective-permute-start.15 = (bf16[3,64,1536]{2,1,0:T(8,128)(2,1)}, bf16[3,64,1536]{2,1,0:T(8,128)(2,1)}, u32[]{:S(2)}, u32[]{:S(2)}) collective-permute-start(bf16[3,64,1536]{2,1,0:T(8,128)(2,1)} %pair_sum.8.refs_5_), channel_id=1, source_target_pairs={{0,2},{1,3},{2,0},{3,1},{4,6},{5,7},{6,4},{7,5},{8,10},{9,11},{10,... | collective-permute-start | bytes 1769480 | tf_op jit(solution)/shard_map/ppermute | solution.py:396
  118.0 10.7 %collective-permute-start.14 = (bf16[2,64,1280]{2,1,0:T(8,128)(2,1)}, bf16[2,64,1280]{2,1,0:T(8,128)(2,1)}, u32[]{:S(2)}, u32[]{:S(2)}) collective-permute-start(bf16[2,64,1280]{2,1,0:T(8,128)(2,1)} %collective-permute-done.12.refs_1_), channel_id=1, source_target_pairs={{0,1},{1,0},{2,3},{3,2},{4,5},{5,4},{6,7},{7,6},{8,9},{9,8},{10,11... | collective-permute-start | bytes 983048 | tf_op jit(solution)/shard_map/ppermute | solution.py:392
  120.4 0.7 copy-start.17
  121.2 26.8 %collective-permute-start.22 = (bf16[2,64,2048]{2,1,0:T(8,128)(2,1)}, bf16[2,64,2048]{2,1,0:T(8,128)(2,1)}, u32[]{:S(2)}, u32[]{:S(2)}) collective-permute-start(bf16[2,64,2048]{2,1,0:T(8,128)(2,1)} %hidden_gradients.7.rest_0_.refs_0_), channel_id=1, source_target_pairs={{0,2},{1,3},{2,0},{3,1},{4,6},{5,7},{6,4},{7,5},{8,10},{9,11},{10,... | collective-permute-start | bytes 1572872 | tf_op jit(solution)/shard_map/ppermute | solution.py:396
  124.6 25.3 %collective-permute-start.10 = (bf16[2,64,1536]{2,1,0:T(8,128)(2,1)}, bf16[2,64,1536]{2,1,0:T(8,128)(2,1)}, u32[]{:S(2)}, u32[]{:S(2)}) collective-permute-start(bf16[2,64,1536]{2,1,0:T(8,128)(2,1)} %get-tuple-element.35.rest_0_.refs_0_), channel_id=1, source_target_pairs={{0,1},{1,0},{2,3},{3,2},{4,5},{5,4},{6,7},{7,6},{8,9},{9,8},{10,11... | collective-permute-start | bytes 1179656 | tf_op jit(solution)/shard_map/ppermute | solution.py:392
  124.7 0.9 copy-start.10
  125.5 26.3 %collective-permute-start.11 = (bf16[2,64,1536]{2,1,0:T(8,128)(2,1)}, bf16[2,64,1536]{2,1,0:T(8,128)(2,1)}, u32[]{:S(2)}, u32[]{:S(2)}) collective-permute-start(bf16[2,64,1536]{2,1,0:T(8,128)(2,1)} %collective-permute-done.9.refs_1_), channel_id=1, source_target_pairs={{0,1},{1,0},{2,3},{3,2},{4,5},{5,4},{6,7},{7,6},{8,9},{9,8},{10,11... | collective-permute-start | bytes 1179656 | tf_op jit(solution)/shard_map/ppermute | solution.py:392
  126.3 1.1 copy-start.6
  127.4 1.1 copy-start.11
  128.6 19.9 %copy-start.9 = (bf16[3,128,1536]{2,1,0:T(8,128)(2,1)S(1)}, bf16[3,128,1536]{2,1,0:T(8,128)(2,1)}, u32[]{:S(2)}) copy-start(bf16[3,128,1536]{2,1,0:T(8,128)(2,1)} %copy-done.8) | copy-start | bytes 3538948
  128.6 76.3 %collective-permute-start.33 = (bf16[256,2048]{1,0:T(8,128)(2,1)S(1)}, bf16[256,2048]{1,0:T(8,128)(2,1)}, u32[]{:S(2)}, u32[]{:S(2)}) collective-permute-start(bf16[256,2048]{1,0:T(8,128)(2,1)S(1)} %copy-done.3), channel_id=1, source_target_pairs={{0,16},{16,0},{1,17},{17,1},{2,18},{18,2},{3,19},{19,3},{4,20},{20... | collective-permute-start | bytes 3145736 | tf_op jit(solution)/shard_map/ppermute | solution.py:399
  130.5 1.0 copy-start.14
  131.5 1.0 copy-start.18
  148.0 14.3 %collective-permute-start.23 = (bf16[2,64,2048]{2,1,0:T(8,128)(2,1)}, bf16[2,64,2048]{2,1,0:T(8,128)(2,1)S(1)}, u32[]{:S(2)}, u32[]{:S(2)}) collective-permute-start(bf16[2,64,2048]{2,1,0:T(8,128)(2,1)} %hidden_gradients.7.rest_0_.refs_0_), channel_id=1, source_target_pairs={{0,1},{1,0},{2,3},{3,2},{4,5},{5,4},{6,7},{7,6},{8,9},{9,8},{10,11... | collective-permute-start | bytes 1572872 | tf_op jit(solution)/shard_map/ppermute | solution.py:392
  148.0 16.1 %collective-permute-start.24 = (bf16[2,64,2048]{2,1,0:T(8,128)(2,1)}, bf16[2,64,2048]{2,1,0:T(8,128)(2,1)S(1)}, u32[]{:S(2)}, u32[]{:S(2)}) collective-permute-start(bf16[2,64,2048]{2,1,0:T(8,128)(2,1)} %collective-permute-done.22.refs_1_), channel_id=1, source_target_pairs={{0,1},{1,0},{2,3},{3,2},{4,5},{5,4},{6,7},{7,6},{8,9},{9,8},{10,11... | collective-permute-start | bytes 1572872 | tf_op jit(solution)/shard_map/ppermute | solution.py:392
  150.0 12.1 %copy-start.7 = (bf16[3,128,1024]{2,1,0:T(8,128)(2,1)S(1)}, bf16[3,128,1024]{2,1,0:T(8,128)(2,1)}, u32[]{:S(2)}) copy-start(bf16[3,128,1024]{2,1,0:T(8,128)(2,1)} %copy-done.5) | copy-start | bytes 2359300
  150.0 12.1 %copy-start.12 = (bf16[3,128,1024]{2,1,0:T(8,128)(2,1)S(1)}, bf16[3,128,1024]{2,1,0:T(8,128)(2,1)}, u32[]{:S(2)}) copy-start(bf16[3,128,1024]{2,1,0:T(8,128)(2,1)} %copy-done.10) | copy-start | bytes 2359300
  150.0 12.1 %collective-permute-start.8 = (bf16[3,64,1024]{2,1,0:T(8,128)(2,1)S(1)}, bf16[3,64,1024]{2,1,0:T(8,128)(2,1)S(1)}, u32[]{:S(2)}, u32[]{:S(2)}) collective-permute-start(bf16[3,64,1024]{2,1,0:T(8,128)(2,1)S(1)} %pair_sum.9.refs_6_), channel_id=1, source_target_pairs={{0,2},{1,3},{2,0},{3,1},{4,6},{5,7},{6,4},{7,5},{8,10},{9,11},{10,... | collective-permute-start | bytes 1179656 | tf_op jit(solution)/shard_map/ppermute | solution.py:396
  151.8 22.3 %collective-permute-start.19 = (bf16[2,64,1664]{2,1,0:T(8,128)(2,1)S(1)}, bf16[2,64,1664]{2,1,0:T(8,128)(2,1)S(1)}, u32[]{:S(2)}, u32[]{:S(2)}) collective-permute-start(bf16[2,64,1664]{2,1,0:T(8,128)(2,1)S(1)} %hidden_gradients.8.refs_7_.refs_0_), channel_id=1, source_target_pairs={{0,2},{1,3},{2,0},{3,1},{4,6},{5,7},{6,4},{7,5},{8,10},{9,11},{10,... | collective-permute-start | bytes 1277960 | tf_op jit(solution)/shard_map/ppermute | solution.py:396
  159.3 5.0 %copy-start.4 = (f32[256,2048]{1,0:T(8,128)}, f32[256,2048]{1,0:T(8,128)S(1)}, u32[]{:S(2)}) copy-start(f32[256,2048]{1,0:T(8,128)S(1)} %products.6.rest_1_.refs_6_) | copy-start | bytes 6291460
  162.0 12.5 %collective-permute-start.20 = (bf16[2,64,1664]{2,1,0:T(8,128)(2,1)S(1)}, bf16[2,64,1664]{2,1,0:T(8,128)(2,1)S(1)}, u32[]{:S(2)}, u32[]{:S(2)}) collective-permute-start(bf16[2,64,1664]{2,1,0:T(8,128)(2,1)S(1)} %hidden_gradients.8.refs_7_.refs_0_), channel_id=1, source_target_pairs={{0,1},{1,0},{2,3},{3,2},{4,5},{5,4},{6,7},{7,6},{8,9},{9,8},{10,11... | collective-permute-start | bytes 1277960 | tf_op jit(solution)/shard_map/ppermute | solution.py:392
  162.3 13.8 %copy-start.16 = (bf16[2048,64]{0,1:T(8,128)(2,1)S(1)}, bf16[2048,64]{0,1:T(8,128)(2,1)}, u32[]{:S(2)}) copy-start(bf16[2048,64]{0,1:T(8,128)(2,1)} %param.13) | copy-start | bytes 786436
  162.3 13.5 %collective-permute-start.16 = (bf16[2,64,1024]{2,1,0:T(8,128)(2,1)S(1)}, bf16[2,64,1024]{2,1,0:T(8,128)(2,1)S(1)}, u32[]{:S(2)}, u32[]{:S(2)}) collective-permute-start(bf16[2,64,1024]{2,1,0:T(8,128)(2,1)S(1)} %hidden_gradients.9.refs_7_.refs_1_), channel_id=1, source_target_pairs={{0,2},{1,3},{2,0},{3,1},{4,6},{5,7},{6,4},{7,5},{8,10},{9,11},{10,... | collective-permute-start | bytes 786440 | tf_op jit(solution)/shard_map/ppermute | solution.py:396
  164.1 24.8 %collective-permute-start.17 = (bf16[2,64,1024]{2,1,0:T(8,128)(2,1)S(1)}, bf16[2,64,1024]{2,1,0:T(8,128)(2,1)S(1)}, u32[]{:S(2)}, u32[]{:S(2)}) collective-permute-start(bf16[2,64,1024]{2,1,0:T(8,128)(2,1)S(1)} %hidden_gradients.9.refs_7_.refs_1_), channel_id=1, source_target_pairs={{0,1},{1,0},{2,3},{3,2},{4,5},{5,4},{6,7},{7,6},{8,9},{9,8},{10,11... | collective-permute-start | bytes 786440 | tf_op jit(solution)/shard_map/ppermute | solution.py:392
  174.1 1.8 collective-permute-start.21
  175.8 14.2 %collective-permute-start.18 = (bf16[2,64,1024]{2,1,0:T(8,128)(2,1)S(1)}, bf16[2,64,1024]{2,1,0:T(8,128)(2,1)S(1)}, u32[]{:S(2)}, u32[]{:S(2)}) collective-permute-start(bf16[2,64,1024]{2,1,0:T(8,128)(2,1)S(1)} %collective-permute-done.16.refs_2_), channel_id=1, source_target_pairs={{0,1},{1,0},{2,3},{3,2},{4,5},{5,4},{6,7},{7,6},{8,9},{9,8},{10,11... | collective-permute-start | bytes 786440 | tf_op jit(solution)/shard_map/ppermute | solution.py:392
  185.0 12.9 %collective-permute-start.30 = (bf16[256,64]{1,0:T(8,128)(2,1)S(1)}, bf16[256,64]{1,0:T(8,128)(2,1)S(1)}, u32[]{:S(2)}, u32[]{:S(2)}) collective-permute-start(bf16[256,64]{1,0:T(8,128)(2,1)S(1)} %get-tuple-element.44.refs_10_), channel_id=1, source_target_pairs={{0,12},{4,0},{8,4},{12,8},{1,13},{5,1},{9,5},{13,9},{2,14},{6,2},{... | collective-permute-start | bytes 98312 | tf_op jit(solution)/shard_map/ppermute | solution.py:399
  188.8 9.1 %collective-permute-start.29 = (bf16[256,64]{1,0:T(8,128)(2,1)S(1)}, bf16[256,64]{1,0:T(8,128)(2,1)S(1)}, u32[]{:S(2)}, u32[]{:S(2)}) collective-permute-start(bf16[256,64]{1,0:T(8,128)(2,1)S(1)} %get-tuple-element.44.refs_10_), channel_id=1, source_target_pairs={{0,8},{4,12},{8,0},{12,4},{1,9},{5,13},{9,1},{13,5},{2,10},{6,14},... | collective-permute-start | bytes 98312 | tf_op jit(solution)/shard_map/ppermute | solution.py:399
  188.9 15.9 %copy-start.21 = (s32[16]{0:T(128)S(1)}, s32[16]{0:T(128)}, u32[]{:S(2)}) copy-start(s32[16]{0:T(128)} %copy-done.20) | copy-start | bytes 196
  188.9 9.0 %collective-permute-start.28 = (bf16[256,64]{1,0:T(8,128)(2,1)S(1)}, bf16[256,64]{1,0:T(8,128)(2,1)S(1)}, u32[]{:S(2)}, u32[]{:S(2)}) collective-permute-start(bf16[256,64]{1,0:T(8,128)(2,1)S(1)} %get-tuple-element.44.refs_10_), channel_id=1, source_target_pairs={{0,4},{4,8},{8,12},{12,0},{1,5},{5,9},{9,13},{13,1},{2,6},{6,10},{... | collective-permute-start | bytes 98312 | tf_op jit(solution)/shard_map/ppermute | solution.py:399
  190.0 13.5 %collective-permute-start.32 = (bf16[256,65]{1,0:T(8,128)(2,1)S(1)}, bf16[256,65]{1,0:T(8,128)(2,1)S(1)}, u32[]{:S(2)}, u32[]{:S(2)}) collective-permute-start(bf16[256,65]{1,0:T(8,128)(2,1)S(1)} %pad_maximum_fusion.3.refs_9_), channel_id=1, source_target_pairs={{0,16},{16,0},{1,17},{17,1},{2,18},{18,2},{3,19},{19,3},{4,20},{20... | collective-permute-start | bytes 99848 | tf_op jit(solution)/shard_map/ppermute | solution.py:399
  199.1 28.6 %collective-permute-start.31 = (f32[64,2048]{1,0:T(8,128)}, f32[64,2048]{1,0:T(8,128)S(1)}, u32[]{:S(2)}, u32[]{:S(2)}) collective-permute-start(f32[64,2048]{1,0:T(8,128)} %fusion.9), channel_id=1, source_target_pairs={{0,16},{16,0},{1,17},{17,1},{2,18},{18,2},{3,19},{19,3},{4,20},{20... | collective-permute-start | bytes 1572872 | tf_op jit(solution)/shard_map/ppermute | solution.py:399
  199.6 12.7 %collective-permute-start.27 = (bf16[64,2048]{1,0:T(8,128)(2,1)}, bf16[64,2048]{1,0:T(8,128)(2,1)S(1)}, u32[]{:S(2)}, u32[]{:S(2)}) collective-permute-start(bf16[64,2048]{1,0:T(8,128)(2,1)} %get-tuple-element.43), channel_id=1, source_target_pairs={{0,12},{4,0},{8,4},{12,8},{1,13},{5,1},{9,5},{13,9},{2,14},{6,2},{... | collective-permute-start | bytes 786440 | tf_op jit(solution)/shard_map/ppermute | solution.py:399
  202.4 23.5 %collective-permute-start.26 = (bf16[64,2048]{1,0:T(8,128)(2,1)S(1)}, bf16[64,2048]{1,0:T(8,128)(2,1)S(1)}, u32[]{:S(2)}, u32[]{:S(2)}) collective-permute-start(bf16[64,2048]{1,0:T(8,128)(2,1)S(1)} %get-tuple-element.42), channel_id=1, source_target_pairs={{0,8},{4,12},{8,0},{12,4},{1,9},{5,13},{9,1},{13,5},{2,10},{6,14},... | collective-permute-start | bytes 786440 | tf_op jit(solution)/shard_map/ppermute | solution.py:399
  203.5 22.3 %collective-permute-start.25 = (bf16[64,2048]{1,0:T(8,128)(2,1)S(1)}, bf16[64,2048]{1,0:T(8,128)(2,1)}, u32[]{:S(2)}, u32[]{:S(2)}) collective-permute-start(bf16[64,2048]{1,0:T(8,128)(2,1)S(1)} %get-tuple-element.41), channel_id=1, source_target_pairs={{0,4},{4,8},{8,12},{12,0},{1,5},{5,9},{9,13},{13,1},{2,6},{6,10},{... | collective-permute-start | bytes 786440 | tf_op jit(solution)/shard_map/ppermute | solution.py:399
where the time goes:
time: 231 us; the launch traced here: 230 us
  Pallas kernels  99.1 us (43%)
  waiting for transfers between devices  70 us (30%)
  starting transfers between devices  28.5 us (12%)
  matrix products  12.4 us (5%)
  local copies, waits for them, and re-layouts  10.7 us (5%)
  other arithmetic  5.24 us (2%)
  between operations  3.78 us (2%)
    ppermute x10, waiting for transfers between devices, shift_chip(): return lax.ppermute(value, 'tensor', pairs)  53.2 us
    pallas_call x5, Pallas kernels, partial_sums(): pl.pallas_call(kernel, grid_spec=pltpu.PrefetchScalarGridSpec(num_scalar_...  49.7 us
    pallas_call x5, Pallas kernels, products(): pl.pallas_call(kernel, grid_spec=pltpu.PrefetchScalarGridSpec(num_scalar_...  39.9 us
    ppermute x9, waiting for transfers between devices, shift(): lax.ppermute(value, axis, [(i, (i + step) % count) for i in range(count)])  13.6 us
    ppermute x10, starting transfers between devices, shift_chip(): return lax.ppermute(value, 'tensor', pairs)  13 us
    ppermute x9, starting transfers between devices, shift(): lax.ppermute(value, axis, [(i, (i + step) % count) for i in range(count)])  12.7 us
    unnamed x44, local copies, waits for them, and re-layouts  9.38 us
    dot_general x2, matrix products, contract_first(): lax.dot_general(left, right, (((0,), (0,)), ((), ())), preferred_element_...  8.43 us
  transfers between devices with their start and end apart: 34, of which 10 were waited for; matrix products, arithmetic and copies ran while one was open for 7% of the time, Pallas kernels for 24%

commit v1 on v0

v1 whole, which is shorter than its diff:
```python
import jax
import jax.numpy as jnp
from jax import lax
from jax.experimental import pallas as pl
from jax.experimental.pallas import tpu as pltpu
from jax.sharding import PartitionSpec as P


ADAPTER_SCALE = 2.0
SHARES = (5, 6, 8, 6, 4)
UNIT = 256
F32, BF16 = jnp.float32, jnp.bfloat16
ANY = pl.BlockSpec(memory_space=pl.ANY)


def contract_last(left, right):
    return lax.dot_general(
        left, right, (((1,), (1,)), ((), ())), preferred_element_type=F32
    )


def contract_first(left, right):
    return lax.dot_general(
        left, right, (((0,), (0,)), ((), ())), preferred_element_type=F32
    )


def chunk_units(hidden):
    units = pl.cdiv(hidden, UNIT)
    total, spans, left, seen = sum(SHARES), [], units, 0
    for share in SHARES:
        seen += share
        first = units - units * seen // total
        if first < left:
            spans.append((first, left - first))
        left = min(left, first)
    return spans


def params(limit_mib=22):
    return pltpu.CompilerParams(vmem_limit_bytes=limit_mib * 2**20)


def token_shape():
    return jax.ShapeDtypeStruct((8, 128), F32)


def keep_valid(value, axis, valid):
    unit = lax.broadcasted_iota(jnp.int32, value.shape, axis)
    return jnp.where(unit < valid, value, jnp.zeros_like(value))


def partial_sums(places, tokens, cotangent, w_gate, w_up, w_down, span, after, extra=None, limit=22):
    first, count = span
    rows, d_cols = tokens.shape
    hidden = w_gate.shape[0]
    half, n = rows // 2, places.shape[0]
    block = rows // n
    width = 2 * UNIT
    steps = pl.cdiv(count, 2)
    more = 0 if extra is None else extra.shape[1]
    last_units = min(hidden - (first + count - 1) * UNIT, UNIT)

    def kernel(places, *refs):
        sides, weights, refs = refs[:2], refs[2:5], refs[5:]
        kept, sent, token, held, buffers, row_sems, sems = refs[-7:]
        step = pl.program_id(0)

        def row_copy(side, k):
            origin = pl.multiple_of(places[k] * block, block)
            return pltpu.make_async_copy(
                sides[side].at[pl.ds(origin, block)],
                held.at[side, pl.ds(k * block, block)],
                row_sems.at[side, k],
            )

        def piece(k, at, u, use):
            def run(units):
                origin = pl.multiple_of((first + 2 * at + u) * UNIT, UNIT)
                use(
                    pltpu.make_async_copy(
                        weights[k].at[pl.ds(origin, units)],
                        buffers.at[k, at % 2, pl.ds(u * UNIT, units)],
                        sems.at[k, at % 2, u],
                    )
                )

            final = (count - 1) // 2, (count - 1) % 2
            if last_units == UNIT and (u == 0 or count % 2 == 0):
                run(UNIT)
                return
            pl.when(at < steps - 1)(lambda: run(UNIT))
            if u <= final[1]:
                pl.when(at == steps - 1)(lambda: run(last_units if u == final[1] else UNIT))

        def start(k, at, u):
            piece(k, at, u, lambda copy: copy.start())

        def wait(k, at, u):
            piece(k, at, u, lambda copy: copy.wait())

        @pl.when(step == 0)
        def _():
            start(0, 0, 0)
            for k in range(n):
                row_copy(0, k).start()
            start(0, 0, 1)
            start(1, 0, 0)
            start(1, 0, 1)
            for k in range(n):
                row_copy(1, k).start()
            start(2, 0, 0)
            start(2, 0, 1)
            for k in range(n):
                row_copy(0, k).wait()

        @pl.when(step < steps)
        def _():
            for k in range(3):

                @pl.when(step + 1 < steps)
                def _():
                    start(k, step + 1, 0)
                    start(k, step + 1, 1)

                if k == 2:

                    @pl.when(step == 0)
                    def _():
                        for b in range(n):
                            row_copy(1, b).wait()

                wait(k, step, 0)
                wait(k, step, 1)
                part = contract_last(held[k // 2], buffers[k, step % 2])
                if last_units < UNIT or count % 2:
                    valid = (count - 1 - 2 * step) * UNIT + last_units
                    part = keep_valid(part, 1, valid)
                kept[k] = part[:half].astype(BF16)
                sent[k] = part[half:].astype(BF16)
            token[...] = jnp.zeros_like(token)

        if more:

            @pl.when(step == count // 2)
            def _():
                columns = slice(count % 2 * UNIT, count % 2 * UNIT + more)
                for k in range(n):
                    origin = pl.multiple_of(places[k] * block, block)
                    out, row = (kept, k) if k < n // 2 else (sent, k - n // 2)
                    at = slice(row * block, (row + 1) * block)
                    out[0, at, columns] = refs[0][pl.ds(origin, block)]
                for out in (kept, sent):
                    out[1:, :, columns] = jnp.zeros((2, half, more), BF16)

    out = pl.BlockSpec((3, half, width), lambda j, places: (0, 0, j))
    shape = jax.ShapeDtypeStruct((3, half, count * UNIT + more), BF16)
    work = rows * d_cols * count * UNIT
    extras = [] if extra is None else [extra]
    return pl.pallas_call(
        kernel,
        grid_spec=pltpu.PrefetchScalarGridSpec(
            num_scalar_prefetch=1,
            grid=(steps + (more > 0 and count % 2 == 0),),
            in_specs=[ANY] * 5
            + [pl.BlockSpec(e.shape, lambda j, places: (0, 0)) for e in extras]
            + [ANY] * len(after),
            out_specs=[out, out, pl.BlockSpec((8, 128), lambda j, places: (0, 0))],
            scratch_shapes=[
                pltpu.VMEM((2, rows, d_cols), BF16),
                pltpu.VMEM((3, 2, width, d_cols), BF16),
                pltpu.SemaphoreType.DMA((2, n)),
                pltpu.SemaphoreType.DMA((3, 2, 2)),
            ],
        ),
        out_shape=[shape, shape, token_shape()],
        compiler_params=params(limit),
        cost_estimate=pl.CostEstimate(
            flops=6 * work, bytes_accessed=6 * d_cols * count * UNIT, transcendentals=0
        ),
        name="partial_sums",
    )(places, tokens, cotangent, w_gate, w_up, w_down, *extras, *after)


def fetch(sources, buffers, sems):
    copies = [
        pltpu.make_async_copy(source, buffers.at[k], sems.at[k])
        for k, source in enumerate(sources)
    ]
    for copy in copies:
        copy.start()
    for copy in copies:
        copy.wait()


def pair_sum(kept, received, b, block, after):
    width = kept.shape[2]
    rows = pl.ds(b * block, block)

    def kernel(mine, other, *rest):
        out, token, buffers, sems = rest[-4:]
        token[...] = jnp.zeros_like(token)
        fetch([mine.at[:, rows], other.at[:, rows]], buffers, sems)
        out[...] = (buffers[0].astype(F32) + buffers[1].astype(F32)).astype(BF16)

    return pl.pallas_call(
        kernel,
        in_specs=[ANY] * (2 + len(after)),
        out_specs=[pl.BlockSpec(memory_space=pltpu.VMEM)] * 2,
        out_shape=[jax.ShapeDtypeStruct((3, block, width), BF16), token_shape()],
        scratch_shapes=[
            pltpu.VMEM((2, 3, block, width), BF16),
            pltpu.SemaphoreType.DMA((2,)),
        ],
        compiler_params=params(),
        cost_estimate=pl.CostEstimate(
            flops=3 * block * width, bytes_accessed=18 * block * width, transcendentals=0
        ),
        name="pair_sum",
    )(kept, received, *after)


def hidden_gradients(kept, received, others, width, block, after, extra=None):
    full = kept.shape[2]
    more = 0 if extra is None else extra.shape[1]
    parts = 2 + len(others)
    outputs = 1 + (full > width)
    extras = [] if extra is None else [extra]

    def kernel(*refs):
        outs, (token, buffers, sems) = refs[-3 - outputs : -3], refs[-3:]
        token[...] = jnp.zeros_like(token)
        mine = pl.ds(0, block)
        fetch(
            [refs[0].at[:, mine], refs[1].at[:, mine], *refs[2:parts]], buffers, sems
        )

        def total(k, columns):
            value = buffers[0, k, :, columns].astype(F32)
            for part in range(1, parts):
                value = value + buffers[part, k, :, columns].astype(F32)
            return value

        for start in range(0, width, UNIT):
            columns = slice(start, start + UNIT)
            gate_pre, up_pre, back = (total(k, columns) for k in range(3))
            sig = jax.nn.sigmoid(gate_pre)
            scaled = back * sig
            grad = scaled * up_pre * (1.0 + gate_pre * (1.0 - sig))
            outs[0][0, :, columns] = grad.astype(BF16)
            outs[0][1, :, columns] = (scaled * gate_pre).astype(BF16)
        if full > width:
            outs[1][...] = total(0, slice(width, full)).astype(BF16)
        if more:
            outs[0][0, :, width:] = refs[parts][...]
            outs[0][1, :, width:] = jnp.zeros((block, more), BF16)

    vmem = pl.BlockSpec(memory_space=pltpu.VMEM)
    return pl.pallas_call(
        kernel,
        in_specs=[ANY] * parts + [vmem] * len(extras) + [ANY] * len(after),
        out_specs=[vmem] * (outputs + 1),
        out_shape=[
            jax.ShapeDtypeStruct((2, block, width + more), BF16),
            jax.ShapeDtypeStruct((block, full - width), BF16),
        ][:outputs]
        + [token_shape()],
        scratch_shapes=[
            pltpu.VMEM((parts, 3, block, full), BF16),
            pltpu.SemaphoreType.DMA((parts,)),
        ],
        compiler_params=params(),
        cost_estimate=pl.CostEstimate(
            flops=20 * block * width, bytes_accessed=22 * block * width,
            transcendentals=block * width,
        ),
        name="hidden_gradients",
    )(kept, received, *others, *extras, *after)


def products(groups, w_gate, w_up, total, after, columns, places=None, factor=None):
    left, wide = columns
    hidden = w_gate.shape[0]
    n = len(groups[0][1])
    block = groups[0][1][0].shape[1]
    rows = block * n
    step_units = 2 if all(span[1] % 2 == 0 for span, _ in groups) else 1
    width = step_units * UNIT
    bounds = [0]
    for span, _ in groups:
        bounds.append(bounds[-1] + span[1] // step_units)
    steps = bounds[-1]
    ragged = [
        min(hidden - (span[0] + span[1]) * UNIT + width, width) for span, _ in groups
    ]
    picks = 0 if places is None else places.shape[0]
    more = 0 if factor is None else factor.shape[0]
    before = [] if total is None else [total]
    factors = [] if factor is None else [factor]

    def kernel(*refs):
        if picks:
            places, refs = refs[0], refs[1:]
        parts = [refs[n * g : n * (g + 1)] for g in range(len(groups))]
        refs = refs[n * len(groups) :]
        weights, refs = refs[:2], refs[2:]
        value, tiles, grads, codes_buffer, tile_sems, grad_sems, sems = refs[-7:]
        outs = refs[: -7][len(before) + len(factors) + len(after) :]
        step = pl.program_id(0)

        def in_group(at, use):
            for g, (span, _) in enumerate(groups):
                local = at - bounds[g]
                inside = jnp.logical_and(at >= bounds[g], at < bounds[g + 1])
                if ragged[g] == width:
                    pl.when(inside)(lambda: use(g, local, width))
                else:
                    is_last = at == bounds[g + 1] - 1
                    pl.when(jnp.logical_and(inside, is_last))(
                        lambda: use(g, local, ragged[g])
                    )
                    pl.when(jnp.logical_and(inside, jnp.logical_not(is_last)))(
                        lambda: use(g, local, width)
                    )

        def tile(k, at, act):
            def use(g, local, units):
                origin = pl.multiple_of(groups[g][0][0] * UNIT + local * width, UNIT)
                act(
                    pltpu.make_async_copy(
                        weights[k].at[pl.ds(origin, units), pl.ds(left, wide)],
                        tiles.at[k, at % 2, pl.ds(0, units)],
                        tile_sems.at[k, at % 2],
                    )
                )

            in_group(at, use)

        def gradient(at, act):
            def use(g, local, units):
                origin = pl.multiple_of(local * width, UNIT)
                for p in range(n):
                    act(
                        pltpu.make_async_copy(
                            parts[g][p].at[:, :, pl.ds(origin, width)],
                            grads.at[at % 2, :, pl.ds(p * block, block)],
                            grad_sems.at[at % 2, p],
                        )
                    )

            in_group(at, use)

        def begin(copy):
            copy.start()

        def end(copy):
            copy.wait()

        def code_copy(p):
            origin = groups[0][0][1] * UNIT
            return pltpu.make_async_copy(
                parts[0][p].at[0, :, pl.ds(origin, more)],
                codes_buffer.at[pl.ds(p * block, block)],
                sems.at[p],
            )

        def total_copy():
            return pltpu.make_async_copy(
                refs[0].at[:, pl.ds(left, wide)], value, sems.at[n]
            )

        @pl.when(step == 0)
        def _():
            gradient(0, begin)
            tile(0, 0, begin)
            if before:
                total_copy().start()
            tile(1, 0, begin)
            if more:
                for p in range(n):
                    code_copy(p).start()
            if before:
                total_copy().wait()
            else:
                value[...] = jnp.zeros_like(value)

        @pl.when(step + 1 < steps)
        def _():
            gradient(step + 1, begin)
            tile(0, step + 1, begin)

        gradient(step, end)
        result = value[...]
        for k in range(2):
            if k == 1:
                pl.when(step + 1 < steps)(lambda: tile(1, step + 1, begin))
            tile(k, step, end)
            part = tiles[k, step % 2]
            if any(r < width for r in ragged):
                valid = jnp.int32(width)
                for g, r in enumerate(ragged):
                    valid = jnp.where(step == bounds[g + 1] - 1, r, valid)
                part = keep_valid(part, 0, valid)
            result = result + jnp.dot(
                grads[step % 2, k], part, preferred_element_type=F32
            )
        value[...] = result

        if more:

            @pl.when(step == steps - 1)
            def _():
                for p in range(n):
                    code_copy(p).wait()
                outs[-1][...] = codes_buffer[...]
                value[...] += jnp.dot(
                    codes_buffer[...], refs[len(before)][:, left : left + wide],
                    preferred_element_type=F32,
                )

        @pl.when(step == steps - 1)
        def _():
            outs[0][...] = jnp.zeros_like(outs[0])
            if picks:
                for k in range(picks):
                    origin = pl.multiple_of(places[k] * block, block)
                    out = outs[1 + k]
                    out[...] = value[pl.ds(origin, block)].astype(out.dtype)
            else:
                outs[1][...] = value[...]

    def whole(shape):
        return pl.BlockSpec(shape, lambda j, *_: (0,) * len(shape))

    work = rows * wide * steps * width
    if picks:
        out_shape = [
            jax.ShapeDtypeStruct((block, wide), BF16 if k else F32) for k in range(picks)
        ]
    else:
        out_shape = [jax.ShapeDtypeStruct((rows, wide), F32)]
    out_shape = [token_shape()] + out_shape
    if more:
        out_shape = out_shape + [jax.ShapeDtypeStruct((rows, more), BF16)]
    flat = [part for _, parts in groups for part in parts]
    return pl.pallas_call(
        kernel,
        grid_spec=pltpu.PrefetchScalarGridSpec(
            num_scalar_prefetch=1 if picks else 0,
            grid=(steps,),
            in_specs=[ANY] * (len(flat) + 2 + len(before))
            + [whole(f.shape) for f in factors]
            + [ANY] * len(after),
            out_specs=[whole(shape.shape) for shape in out_shape],
            scratch_shapes=[
                pltpu.VMEM((rows, wide), F32),
                pltpu.VMEM((2, 2, width, wide), BF16),
                pltpu.VMEM((2, 2, rows, width), BF16),
                pltpu.VMEM((rows, max(more, 128)), BF16),
                pltpu.SemaphoreType.DMA((2, 2)),
                pltpu.SemaphoreType.DMA((2, n)),
                pltpu.SemaphoreType.DMA((n + 1,)),
            ],
        ),
        out_shape=out_shape,
        compiler_params=params(),
        cost_estimate=pl.CostEstimate(
            flops=4 * work, bytes_accessed=4 * wide * steps * width, transcendentals=0
        ),
        name="products",
    )(*([places] if picks else []), *flat, w_gate, w_up, *before, *factors, *after)


def adapter_columns(tokens, cotangent, factor, heads, places, after):
    rows, d_cols = tokens.shape
    rank = factor.shape[0]
    width = min(4 * rank, heads.shape[0])
    steps = heads.shape[0] // width

    def kernel(tok, cot, down, up, head, *rest):
        out, token, total = rest[-3:]
        step = pl.program_id(0)

        @pl.when(step == 0)
        def _():
            token[...] = jnp.zeros_like(token)
            total[...] = jnp.zeros_like(total)
            out[:, :rank] = contract_last(tok[...], down[...]).astype(BF16)

        separated = contract_last(cot[...], up[...])
        column = lax.broadcasted_iota(jnp.int32, separated.shape, 1)
        chosen = step * (width // rank) + column // rank == head[...]
        part = jnp.where(chosen, ADAPTER_SCALE * separated, 0.0).astype(BF16)
        row = lax.broadcasted_iota(jnp.int32, (width, rank), 0)
        fold = row % rank == lax.broadcasted_iota(jnp.int32, (width, rank), 1)
        total[...] += jnp.dot(part, fold.astype(BF16), preferred_element_type=F32)

        @pl.when(step == steps - 1)
        def _():
            out[:, rank:] = total[...].astype(BF16)

    def whole(shape):
        return pl.BlockSpec(shape, lambda j: (0, 0))

    return pl.pallas_call(
        kernel,
        grid=(steps,),
        in_specs=[
            whole(tokens.shape),
            whole(tokens.shape),
            whole(factor.shape),
            pl.BlockSpec((width, d_cols), lambda j: (j, 0)),
            whole(places.shape),
        ]
        + [ANY] * len(after),
        out_specs=[whole((rows, 2 * rank)), whole((8, 128))],
        out_shape=[jax.ShapeDtypeStruct((rows, 2 * rank), BF16), token_shape()],
        scratch_shapes=[pltpu.VMEM((rows, rank), F32)],
        compiler_params=params(),
        cost_estimate=pl.CostEstimate(
            flops=2 * rows * d_cols * (rank + heads.shape[0]),
            bytes_accessed=2 * d_cols * heads.shape[0],
            transcendentals=0,
        ),
        name="adapter_columns",
    )(tokens, cotangent, factor, heads, places, *after)


def gather_columns(places, parts, start, after):
    n, block = len(parts), parts[0].shape[1]
    more = parts[0].shape[2] - start

    def kernel(places, *refs):
        out, token, buffer, sems = refs[-4:]
        token[...] = jnp.zeros_like(token)
        copies = [
            pltpu.make_async_copy(
                refs[k].at[0, :, pl.ds(start, more)], buffer.at[k], sems.at[k]
            )
            for k in range(n)
        ]
        for copy in copies:
            copy.start()
        for copy in copies:
            copy.wait()
        for k in range(n):
            origin = pl.multiple_of(places[k] * block, block)
            out[pl.ds(origin, block)] = buffer[k]

    shape = jax.ShapeDtypeStruct((n * block, more), BF16)
    return pl.pallas_call(
        kernel,
        grid_spec=pltpu.PrefetchScalarGridSpec(
            num_scalar_prefetch=1,
            grid=(1,),
            in_specs=[ANY] * (n + len(after)),
            out_specs=[
                pl.BlockSpec(shape.shape, lambda j, places: (0, 0)),
                pl.BlockSpec((8, 128), lambda j, places: (0, 0)),
            ],
            scratch_shapes=[
                pltpu.VMEM((n, block, more), BF16),
                pltpu.SemaphoreType.DMA((n,)),
            ],
        ),
        out_shape=[shape, token_shape()],
        compiler_params=params(),
        name="gather_columns",
    )(places, *parts, *after)


def ordered(value, *earlier):
    return lax.optimization_barrier((value, *earlier))[0]


def backward(tokens, cotangent, w_gate, w_up, w_down, common_down_factor, head_up, routes):
    tok_rows, d_cols = tokens.shape
    hidden = w_gate.shape[1]
    rank = common_down_factor.shape[1]
    local_heads = head_up.shape[0]
    n_tensor, n_head, n_dp = (lax.axis_size(a) for a in ("tensor", "head", "dp"))
    chips = n_tensor // 2
    me = lax.axis_index("tensor")
    my_chip, my_core = me // 2, me % 2
    my_head, my_dp = lax.axis_index("head"), lax.axis_index("dp")
    block = tok_rows // n_tensor
    out_rows = tok_rows // n_head
    if out_rows != block or n_tensor % 2:
        raise ValueError("unsupported mesh")

    def place_of(owner):
        core, chip = owner // chips, owner % chips
        return (core + my_core) % 2 * chips + (chip - my_chip) % chips

    order = jnp.arange(n_tensor, dtype=jnp.int32)
    places = (order // chips + my_core) % 2 * chips + (order % chips + my_chip) % chips

    def swap_core(value):
        return lax.ppermute(value, "tensor", [(i, i ^ 1) for i in range(n_tensor)])

    def shift_chip(value, step):
        pairs = [(i, (i // 2 + step) % chips * 2 + i % 2) for i in range(n_tensor)]
        return lax.ppermute(value, "tensor", pairs)

    def shift(value, axis, count, step):
        return lax.ppermute(value, axis, [(i, (i + step) % count) for i in range(count)])

    head_ids = my_head * local_heads + jnp.arange(local_heads, dtype=jnp.int32)[None, :]

    spans = chunk_units(hidden)
    count = len(spans)
    w_gate, w_up = w_gate.T, w_up.T
    sums, grads, after = [], [], []
    adapter = {}

    def finish(c, after):
        kept, received, others = sums[c]
        own, *rest, token = hidden_gradients(
            kept, received, others, spans[c][1] * UNIT, block, after,
            adapter["own"] if c == 2 else None,
        )
        if c == 1:
            adapter["own"] = rest[0]
        near = swap_core(own)
        far = [shift_chip(own, -b) for b in range(1, chips)]
        grads.append([own] + far + [near] + [swap_core(f) for f in far])
        return token

    other_cotangents = [shift(cotangent, "dp", n_dp, s) for s in range(1, n_dp)]

    for c, span in enumerate(spans):
        kept, sent, token = partial_sums(
            places, tokens, cotangent, w_gate, w_up, w_down, span, after,
            adapter["part"] if c == 1 else None, 60 if c == 0 else 22,
        )
        received = swap_core(sent)
        after = [token]
        if c == 0:
            adapter["part"], token = adapter_columns(
                tokens, cotangent, common_down_factor.T,
                head_up.reshape(local_heads * rank, d_cols),
                routes - my_head * local_heads, after,
            )
            after = [token]
        if c >= 2:
            after = [finish(c - 2, after)]
        pairs = [pair_sum(kept, received, b, block, after) for b in range(1, chips)]
        others = [shift_chip(p, b + 1) for b, (p, _) in enumerate(pairs)]
        sums.append((kept, received, others))
        after = [token for _, token in pairs]

    total = None
    head_places = place_of((my_head + jnp.arange(n_head, dtype=jnp.int32)) % n_head)
    for c in range(count - 2):
        token, total = products(
            [(spans[c], grads[c])], w_gate, w_up, total, after, (0, d_cols)
        )
        after = [token]
        if c >= count - 4:
            after = [finish(len(grads), after)]

    both, token = gather_columns(places, grads[2], spans[2][1] * UNIT, after)
    after = [token]
    codes = jnp.concatenate([both[:, :rank], routes.astype(BF16)], axis=1)
    part = both[:, rank:]
    other_codes = [shift(codes, "dp", n_dp, s) for s in range(1, n_dp)]
    head_parts = [shift(part, "head", n_head, s) for s in range(1, n_head)]

    code_grad = ordered(part, token).astype(F32)
    for other in head_parts:
        code_grad = code_grad + other.astype(F32)
    code_grad = code_grad.astype(BF16)
    shared = contract_first(code_grad, tokens)
    other_shared = [shift(shared, "dp", n_dp, s) for s in range(1, n_dp)]

    own_rows, received = [], []
    wide = d_cols // 2
    for side in range(2):
        token, own, *sends = products(
            list(zip(spans[-2:], grads[-2:])), w_gate, w_up, total, after,
            (side * wide, wide), head_places,
        )
        after = [token]
        own_rows.append(own)
        received.append(
            [shift(send, "head", n_head, s + 1) for s, send in enumerate(sends)]
        )

    def by_group(own, others):
        doubled = jnp.concatenate([own] + others[::-1], axis=0)
        doubled = jnp.concatenate([doubled, doubled], axis=0)
        count = own.shape[0]
        start = (n_dp - my_dp) % n_dp * count
        return lax.dynamic_slice_in_dim(doubled, start, n_dp * count, 0)

    all_codes = by_group(ordered(codes, token), other_codes)
    all_cotangents = by_group(ordered(cotangent, token), other_cotangents)
    masked = jnp.where(
        (all_codes[:, rank:].astype(jnp.int32) == head_ids)[:, :, None],
        all_codes[:, None, :rank],
        jnp.zeros((), BF16),
    ).reshape(n_dp * tok_rows, local_heads * rank)
    up_heads = ADAPTER_SCALE * contract_first(masked, all_cotangents)
    up_heads = up_heads.reshape(local_heads, rank, d_cols)

    grad_shared = ordered(shared, token)
    for other in other_shared:
        grad_shared = grad_shared + other
    grad_shared = grad_shared.T

    own_code_grad = lax.dynamic_slice_in_dim(code_grad, my_head * out_rows, out_rows, 0)
    adapter_rows = contract_last(own_code_grad, common_down_factor)
    halves = []
    for side, (own, others) in enumerate(zip(own_rows, received)):
        own = own + adapter_rows[:, side * wide : (side + 1) * wide]
        for other in others:
            own = own + other.astype(F32)
        halves.append(own.astype(BF16))
    return jnp.concatenate(halves, axis=1), grad_shared, up_heads


def solution(mesh):
    placed = (
        P("dp", "tensor"),
        P("dp", "tensor"),
        P("tensor", "head"),
        P("tensor", "head"),
        P("head", "tensor"),
        P("tensor", None),
        P("head", None, "tensor"),
        P("dp", None),
    )
    return jax.shard_map(
        backward,
        mesh=mesh,
        in_specs=placed,
        out_specs=(P(("dp", "head"), "tensor"), P("tensor", None), P("head", None, "tensor")),
        check_vma=False,
    )
```

time: 231 us -> 233 us (level)
  starting transfers between devices: 28.5 us -> 34.6 us
  matrix products: 12.4 us -> 8.68 us
  local copies, waits for them, and re-layouts: 10.7 us -> 13.6 us
  between operations: 3.78 us -> 1.22 us
    ppermute x9 -> x12, starting transfers between devices: 12.7 us -> 18.1 us  [shift(): lax.ppermute(value, axis, [(i, (i + step) % count) for i in range(count)])]
    unnamed x44 -> x53, local copies, waits for them, and re-layouts: 9.38 us -> 13.3 us
    pallas_call x10 -> x12, Pallas kernels: 9.43 us -> 12.8 us  [the longest x5 5.86 us: hidden_gradients(): pl.pallas_call(kernel, in_specs=[ANY] * parts + [vmem] * len(extras) + [A...]
    ppermute x10, waiting for transfers between devices: 53.2 us -> 56.5 us  [shift_chip(): return lax.ppermute(value, 'tensor', pairs)]
    ppermute x9 -> x12, waiting for transfers between devices: 13.6 us -> 10.8 us  [shift(): lax.ppermute(value, axis, [(i, (i + step) % count) for i in range(count)])]
    dot_general x1, matrix products: 3.48 us -> 1.02 us  [contract_last(): lax.dot_general(left, right, (((1,), (1,)), ((), ())), preferred_element_...]
  transfers between devices with their start and end apart: 34 -> 37, of which waited for: 10 -> 11; matrix products, arithmetic and copies ran while one was open for 7% -> 5% of each run, Pallas kernels for 24% -> 25%
where the time goes in v1:
time: 233 us; the launch traced here: 232 us
  Pallas kernels  98.9 us (42%)
  waiting for transfers between devices  70.2 us (30%)
  starting transfers between devices  34.6 us (15%)
  local copies, waits for them, and re-layouts  13.6 us (6%)
  matrix products  8.68 us (4%)
  other arithmetic  4.74 us (2%)
    ppermute x10, waiting for transfers between devices, shift_chip(): return lax.ppermute(value, 'tensor', pairs)  56.5 us
    pallas_call x5, Pallas kernels, partial_sums(): pl.pallas_call(kernel, grid_spec=pltpu.PrefetchScalarGridSpec(num_scalar_...  47.8 us
    pallas_call x5, Pallas kernels, products(): pl.pallas_call(kernel, grid_spec=pltpu.PrefetchScalarGridSpec(num_scalar_...  38.3 us
    ppermute x12, starting transfers between devices, shift(): lax.ppermute(value, axis, [(i, (i + step) % count) for i in range(count)])  18.1 us
    unnamed x53, local copies, waits for them, and re-layouts  13.3 us
    ppermute x10, starting transfers between devices, shift_chip(): return lax.ppermute(value, 'tensor', pairs)  13.1 us
    ppermute x12, waiting for transfers between devices, shift(): lax.ppermute(value, axis, [(i, (i + step) % count) for i in range(count)])  10.8 us
    dot_general x2, matrix products, contract_first(): lax.dot_general(left, right, (((0,), (0,)), ((), ())), preferred_element_...  7.66 us
  transfers between devices with their start and end apart: 37, of which 11 were waited for; matrix products, arithmetic and copies ran while one was open for 5% of the time, Pallas kernels for 25%

profile of v1, /device:TPU:0, one launch (start us, length us, event | category | flops | bytes accessed | tf_op | source)
XLA Modules:
  0.0 232.0 jit_solution(5459201250301314762)
XLA Ops:
  1.2 10.5 %partial_sums.5 = (bf16[3,128,1280]{2,1,0:T(8,128)(2,1)}, bf16[3,128,1280]{2,1,0:T(8,128)(2,1)}, f32[8,128]{1,0:T(8,128)}) custom-call(s32[4]{0:T(128)} %fusion.21.places, bf16[256,2048]{1,0:T(8,128)(2,1)} %refs_0_.9, bf16[256,2048]{1,0:T(8,128)(2,1)} %refs_1_.9, bf16[7392,2048]{1,0:T(8,128)(2,1)} %bitcast.15, bf16[7392,2048]{1,0:T(8,128)(2,1)} %bitcast.25, ...), custom_call_target="tpu_custom_call" | custom-call | flops 4026531840 | bytes 15728640 | tf_op jit(solution)/shard_map/partial_sums/pallas_call | solution.py:160
  11.7 1.4 collective-permute-start
  13.3 2.2 copy-done.4
  15.5 0.7 copy-done.23
  16.1 3.2 %adapter_columns.1 = (bf16[256,128]{1,0:T(8,128)(2,1)S(1)}, f32[8,128]{1,0:T(8,128)S(1)}) custom-call(bf16[256,2048]{1,0:T(8,128)(2,1)S(1)} %copy-done, bf16[256,2048]{1,0:T(8,128)(2,1)S(1)} %copy-done.1, bf16[64,2048]{1,0:T(8,128)(2,1)S(1)} %bitcast.14, bf16[1024,2048]{1,0:T(8,128)(2,1)S(1)} %bitcast.13, s32[256,1]{1,0:T(8,128)S(1)} %broadcast_subtract_fusion.head, ...), custom_call_target="tpu_custom_call" | custom-call | flops 1140850688 | bytes 4194304 | tf_op jit(solution)/shard_map/adapter_columns/pallas_call | solution.py:505
  19.7 9.5 %partial_sums.6 = (bf16[3,128,1664]{2,1,0:T(8,128)(2,1)S(1)}, bf16[3,128,1664]{2,1,0:T(8,128)(2,1)S(1)}, f32[8,128]{1,0:T(8,128)S(1)}) custom-call(s32[4]{0:T(128)S(1)} %copy-done.22, bf16[256,2048]{1,0:T(8,128)(2,1)S(1)} %copy-done, bf16[256,2048]{1,0:T(8,128)(2,1)S(1)} %copy-done.1, bf16[7392,2048]{1,0:T(8,128)(2,1)} %bitcast.16, ...), custom_call_target="tpu_custom_call" | custom-call | flops 4831838208 | bytes 18874368 | tf_op jit(solution)/shard_map/partial_sums/pallas_call | solution.py:160
  29.4 3.0 %collective-permute-done.1.other.refs_1_ = bf16[3,128,1664]{2,1,0:T(8,128)(2,1)S(1)} collective-permute-done((bf16[3,128,1664]{2,1,0:T(8,128)(2,1)S(1)}, bf16[3,128,1664]{2,1,0:T(8,128)(2,1)S(1)}, u32[]{:S(2)}, u32[]{:S(2)}) %collective-permute-start.1) | collective-permute-done | bytes 1277984 | tf_op jit(solution)/shard_map/ppermute | solution.py:599
  32.6 11.5 %partial_sums.7 = (bf16[3,128,2048]{2,1,0:T(8,128)(2,1)S(1)}, bf16[3,128,2048]{2,1,0:T(8,128)(2,1)S(1)}, f32[8,128]{1,0:T(8,128)S(1)}) custom-call(s32[4]{0:T(128)S(1)} %copy-done.22, bf16[256,2048]{1,0:T(8,128)(2,1)S(1)} %copy-done, bf16[256,2048]{1,0:T(8,128)(2,1)S(1)} %copy-done.1, bf16[7392,2048]{1,0:T(8,128)(2,1)} %bitcast.17, ...), custom_call_target="tpu_custom_call" | custom-call | flops 6442450944 | bytes 25165824 | tf_op jit(solution)/shard_map/partial_sums/pallas_call | solution.py:160
  44.3 3.0 %collective-permute-start.3 = (bf16[3,64,1280]{2,1,0:T(8,128)(2,1)S(1)}, bf16[3,64,1280]{2,1,0:T(8,128)(2,1)S(1)}, u32[]{:S(2)}, u32[]{:S(2)}) collective-permute-start(bf16[3,64,1280]{2,1,0:T(8,128)(2,1)S(1)} %get-tuple-element.75), channel_id=1, source_target_pairs={{0,2},{1,3},{2,0},{3,1},{4,6},{5,7},{6,4},{7,5},{8,10},{9,11},{10,... | collective-permute-start | bytes 1474568 | tf_op jit(solution)/shard_map/ppermute | solution.py:603
  47.4 11.8 %collective-permute-done.3.refs_2_ = bf16[3,64,1280]{2,1,0:T(8,128)(2,1)S(1)} collective-permute-done((bf16[3,64,1280]{2,1,0:T(8,128)(2,1)S(1)}, bf16[3,64,1280]{2,1,0:T(8,128)(2,1)S(1)}, u32[]{:S(2)}, u32[]{:S(2)}) %collective-permute-start.3) | collective-permute-done | bytes 491552 | tf_op jit(solution)/shard_map/ppermute | solution.py:603
  59.1 0.8 hidden_gradients.5
  60.5 9.2 %partial_sums.8 = (bf16[3,128,1536]{2,1,0:T(8,128)(2,1)S(1)}, bf16[3,128,1536]{2,1,0:T(8,128)(2,1)S(1)}, f32[8,128]{1,0:T(8,128)S(1)}) custom-call(s32[4]{0:T(128)S(1)} %copy-done.22, bf16[256,2048]{1,0:T(8,128)(2,1)S(1)} %copy-done, bf16[256,2048]{1,0:T(8,128)(2,1)S(1)} %copy-done.1, bf16[7392,2048]{1,0:T(8,128)(2,1)} %bitcast.18, ...), custom_call_target="tpu_custom_call" | custom-call | flops 4831838208 | bytes 18874368 | tf_op jit(solution)/shard_map/partial_sums/pallas_call | solution.py:160
  69.7 1.8 collective-permute-start.5
  71.8 15.2 %collective-permute-done.5.refs_2_ = bf16[3,64,1664]{2,1,0:T(8,128)(2,1)S(1)} collective-permute-done((bf16[3,64,1664]{2,1,0:T(8,128)(2,1)S(1)}, bf16[3,64,1664]{2,1,0:T(8,128)(2,1)S(1)}, u32[]{:S(2)}, u32[]{:S(2)}) %collective-permute-start.5) | collective-permute-done | bytes 639008 | tf_op jit(solution)/shard_map/ppermute | solution.py:603
  87.1 1.4 hidden_gradients.6
  88.5 1.1 pair_sum.8
  89.5 1.0 copy-done.2
  90.5 7.1 %partial_sums.9 = (bf16[3,128,1024]{2,1,0:T(8,128)(2,1)S(1)}, bf16[3,128,1024]{2,1,0:T(8,128)(2,1)S(1)}, f32[8,128]{1,0:T(8,128)S(1)}) custom-call(s32[4]{0:T(128)S(1)} %copy-done.22, bf16[256,2048]{1,0:T(8,128)(2,1)S(1)} %copy-done, bf16[256,2048]{1,0:T(8,128)(2,1)S(1)} %copy-done.1, bf16[7392,2048]{1,0:T(8,128)(2,1)} %bitcast.19, ...), custom_call_target="tpu_custom_call" | custom-call | flops 3221225472 | bytes 12582912 | tf_op jit(solution)/shard_map/partial_sums/pallas_call | solution.py:160
  97.7 1.8 collective-permute-start.10
  99.5 4.4 %collective-permute-done.14.refs_2_ = bf16[3,64,2048]{2,1,0:T(8,128)(2,1)S(1)} collective-permute-done((bf16[3,64,2048]{2,1,0:T(8,128)(2,1)S(1)}, bf16[3,64,2048]{2,1,0:T(8,128)(2,1)S(1)}, u32[]{:S(2)}, u32[]{:S(2)}) %collective-permute-start.14) | collective-permute-done | bytes 786464 | tf_op jit(solution)/shard_map/ppermute | solution.py:603
  103.9 1.6 hidden_gradients.7
  105.5 1.8 collective-permute-start.19
  107.6 3.3 %collective-permute-done.10.refs_1_ = bf16[2,64,1280]{2,1,0:T(8,128)(2,1)S(1)} collective-permute-done((bf16[2,64,1280]{2,1,0:T(8,128)(2,1)S(1)}, bf16[2,64,1280]{2,1,0:T(8,128)(2,1)S(1)}, u32[]{:S(2)}, u32[]{:S(2)}) %collective-permute-start.10) | collective-permute-done | bytes 327712 | tf_op jit(solution)/shard_map/ppermute | solution.py:603
  110.9 0.7 copy-done.16
  111.7 0.8 copy-done.18
  112.9 17.9 %collective-permute-done.7.refs_1_ = bf16[2,64,1536]{2,1,0:T(8,128)(2,1)} collective-permute-done((bf16[2,64,1536]{2,1,0:T(8,128)(2,1)}, bf16[2,64,1536]{2,1,0:T(8,128)(2,1)}, u32[]{:S(2)}, u32[]{:S(2)}) %collective-permute-start.7) | collective-permute-done | bytes 393248 | tf_op jit(solution)/shard_map/ppermute | solution.py:603
  130.9 0.7 copy-done.20
  132.2 1.7 collective-permute-start.6
  133.9 0.9 copy-done.9
  135.0 1.1 copy-done.7
  136.1 1.1 copy-done.10
  137.5 1.0 copy-done.15
  138.4 1.0 copy-done.17
  139.4 1.0 copy-done.19
  140.4 1.0 copy-done.21
  141.4 6.9 %products.5 = (f32[8,128]{1,0:T(8,128)S(1)}, f32[256,2048]{1,0:T(8,128)S(1)}) custom-call(bf16[2,64,1280]{2,1,0:T(8,128)(2,1)S(1)} %copy-done.15, bf16[2,64,1280]{2,1,0:T(8,128)(2,1)S(1)} %copy-done.17, bf16[2,64,1280]{2,1,0:T(8,128)(2,1)S(1)} %copy-done.19, bf16[2,64,1280]{2,1,0:T(8,128)(2,1)S(1)} %copy-done.21, bf16[7392,2048]{1,0:T(8,128)(2,1)} %bitcast.20, ...), custom_call_target="tpu_custom_call" | custom-call | flops 2684354560 | bytes 10485760 | tf_op jit(solution)/shard_map/products/pallas_call | solution.py:446
  148.2 1.6 collective-permute-start.36
  150.1 6.9 %products.6 = (f32[8,128]{1,0:T(8,128)S(1)}, f32[256,2048]{1,0:T(8,128)S(1)}) custom-call(bf16[2,64,1536]{2,1,0:T(8,128)(2,1)} %get-tuple-element.85.refs_0_, bf16[2,64,1536]{2,1,0:T(8,128)(2,1)} %collective-permute-done.7.refs_1_, bf16[2,64,1536]{2,1,0:T(8,128)(2,1)} %collective-permute-done.8.refs_2_, bf16[2,64,1536]{2,1,0:T(8,128)(2,1)} %collective-permute-done.9.refs_3_, ...), custom_call_target="tpu_custom_call" | custom-call | flops 3221225472 | bytes 12582912 | tf_op jit(solution)/shard_map/products/pallas_call | solution.py:446
  157.0 1.5 hidden_gradients.8
  158.5 1.8 collective-permute-start.15
  160.3 8.8 %products.7 = (f32[8,128]{1,0:T(8,128)S(1)}, f32[256,2048]{1,0:T(8,128)S(1)}) custom-call(bf16[2,64,2176]{2,1,0:T(8,128)(2,1)} %get-tuple-element.100.refs_0_, bf16[2,64,2176]{2,1,0:T(8,128)(2,1)} %collective-permute-done.19.refs_1_, bf16[2,64,2176]{2,1,0:T(8,128)(2,1)} %collective-permute-done.20.refs_2_, ...), custom_call_target="tpu_custom_call" | custom-call | flops 4294967296 | bytes 16777216 | tf_op jit(solution)/shard_map/products/pallas_call | solution.py:446
  169.8 1.4 gather_columns.1
  171.2 1.6 collective-permute-start.25
  172.9 2.6 %collective-permute-start.26 = (bf16[256,64]{1,0:T(8,128)(2,1)S(1)}, bf16[256,64]{1,0:T(8,128)(2,1)S(1)}, u32[]{:S(2)}, u32[]{:S(2)}) collective-permute-start(bf16[256,64]{1,0:T(8,128)(2,1)S(1)} %get-tuple-element.110), channel_id=1, source_target_pairs={{0,8},{4,12},{8,0},{12,4},{1,9},{5,13},{9,1},{13,5},{2,10},{6,14},... | collective-permute-start | bytes 98312 | tf_op jit(solution)/shard_map/ppermute | solution.py:606
  175.5 1.3 collective-permute-start.27
  177.0 1.1 collective-permute-done.25
  178.3 1.9 collective-permute-done.26
  180.8 1.0 fusion.15
  181.8 3.9 %collective-permute-done.22.refs_6_ = bf16[2,64,1024]{2,1,0:T(8,128)(2,1)S(1)} collective-permute-done((bf16[2,64,1024]{2,1,0:T(8,128)(2,1)S(1)}, bf16[2,64,1024]{2,1,0:T(8,128)(2,1)S(1)}, u32[]{:S(2)}, u32[]{:S(2)}) %collective-permute-start.22) | collective-permute-done | bytes 262176 | tf_op jit(solution)/shard_map/ppermute | solution.py:603
  186.0 0.6 collective-permute-start.35
  186.6 1.5 collective-permute-start.34
  188.1 7.7 %products.8 = (f32[8,128]{1,0:T(8,128)S(1)}, f32[64,1024]{1,0:T(8,128)S(1)}, bf16[64,1024]{1,0:T(8,128)(2,1)S(1)}, bf16[64,1024]{1,0:T(8,128)(2,1)S(1)}, bf16[64,1024]{1,0:T(8,128)(2,1)S(1)}) custom-call(s32[4]{0:T(128)S(1)} %fusion.19.refs_0_, bf16[2,64,1536]{2,1,0:T(8,128)(2,1)S(1)} %get-tuple-element.98.refs_1_, ...), custom_call_target="tpu_custom_call" | custom-call | flops 2684354560 | bytes 10485760 | tf_op jit(solution)/shard_map/products/pallas_call | solution.py:446
  195.8 8.0 %products.9 = (f32[8,128]{1,0:T(8,128)}, f32[64,1024]{1,0:T(8,128)S(1)}, bf16[64,1024]{1,0:T(8,128)(2,1)S(1)}, bf16[64,1024]{1,0:T(8,128)(2,1)S(1)}, bf16[64,1024]{1,0:T(8,128)(2,1)S(1)}) custom-call(s32[4]{0:T(128)S(1)} %fusion.19.refs_0_, bf16[2,64,1536]{2,1,0:T(8,128)(2,1)S(1)} %get-tuple-element.98.refs_1_, ...), custom_call_target="tpu_custom_call" | custom-call | flops 2684354560 | bytes 10485760 | tf_op jit(solution)/shard_map/products/pallas_call | solution.py:446
  203.9 0.9 fusion.14
  204.9 0.7 collective-permute-start.31
  206.3 7.3 %convolution_multiply_fusion = f32[1024,2048]{1,0:T(8,128)} fusion(bf16[512,1024]{0,1:T(8,128)(2,1)S(1)} %bitcast.36, s32[]{:T(128)S(6)} %select_n.83, bf16[256,2048]{1,0:T(8,128)(2,1)S(1)} %copy-done.1, bf16[256,2048]{1,0:T(8,128)(2,1)} %collective-permute-done.36), kind=kOutput, calls=%fused_computation | convolution fusion | flops 2157969408 | bytes 11534340 | tf_op jit(solution)/shard_map/dot_general | solution.py:23
  213.7 2.8 %collective-permute-start.33 = (bf16[64,1024]{1,0:T(8,128)(2,1)S(1)}, bf16[64,1024]{1,0:T(8,128)(2,1)S(1)}, u32[]{:S(2)}, u32[]{:S(2)}) collective-permute-start(bf16[64,1024]{1,0:T(8,128)(2,1)S(1)} %get-tuple-element.118), channel_id=1, source_target_pairs={{0,12},{4,0},{8,4},{12,8},{1,13},{5,1},{9,5},{13,9},{2,14},{6,2},{... | collective-permute-start | bytes 393224 | tf_op jit(solution)/shard_map/ppermute | solution.py:606
  216.5 0.6 collective-permute-start.28
  217.1 1.5 collective-permute-start.29
  218.5 2.9 %collective-permute-start.30 = (bf16[64,1024]{1,0:T(8,128)(2,1)S(1)}, bf16[64,1024]{1,0:T(8,128)(2,1)S(1)}, u32[]{:S(2)}, u32[]{:S(2)}) collective-permute-start(bf16[64,1024]{1,0:T(8,128)(2,1)S(1)} %get-tuple-element.113), channel_id=1, source_target_pairs={{0,12},{4,0},{8,4},{12,8},{1,13},{5,1},{9,5},{13,9},{2,14},{6,2},{... | collective-permute-start | bytes 393224 | tf_op jit(solution)/shard_map/ppermute | solution.py:606
  221.4 1.9 add_bitcast_fusion
  223.3 1.4 collective-permute-done.28
  224.8 6.3 %collective-permute-done.29 = bf16[64,1024]{1,0:T(8,128)(2,1)S(1)} collective-permute-done((bf16[64,1024]{1,0:T(8,128)(2,1)S(1)}, bf16[64,1024]{1,0:T(8,128)(2,1)S(1)}, u32[]{:S(2)}, u32[]{:S(2)}) %collective-permute-start.29) | collective-permute-done | bytes 131104 | tf_op jit(solution)/shard_map/ppermute | solution.py:606
  231.3 0.7 pad_maximum_fusion
  (105 shorter events, 7.5 us)
Async XLA Ops:
  1.2 11.9 %copy-start.25 = (s32[256,1]{0,1:T(1,128)S(1)}, s32[256,1]{0,1:T(1,128)}, u32[]{:S(2)}) copy-start(s32[256,1]{0,1:T(1,128)} %param.15) | copy-start | bytes 3076
  1.2 12.1 %copy-start = (bf16[256,2048]{1,0:T(8,128)(2,1)S(1)}, bf16[256,2048]{1,0:T(8,128)(2,1)}, u32[]{:S(2)}) copy-start(bf16[256,2048]{1,0:T(8,128)(2,1)} %refs_0_.9) | copy-start | bytes 3145732
  1.2 12.1 %copy-start.1 = (bf16[256,2048]{1,0:T(8,128)(2,1)S(1)}, bf16[256,2048]{1,0:T(8,128)(2,1)}, u32[]{:S(2)}) copy-start(bf16[256,2048]{1,0:T(8,128)(2,1)} %refs_1_.9) | copy-start | bytes 3145732
  1.2 12.1 %copy-start.12 = (bf16[2048,64]{0,1:T(8,128)(2,1)S(1)}, bf16[2048,64]{0,1:T(8,128)(2,1)}, u32[]{:S(2)}) copy-start(bf16[2048,64]{0,1:T(8,128)(2,1)} %param.13) | copy-start | bytes 786436
  11.7 7.6 %collective-permute-start = (bf16[3,128,1280]{2,1,0:T(8,128)(2,1)}, bf16[3,128,1280]{2,1,0:T(8,128)(2,1)S(1)}, u32[]{:S(2)}, u32[]{:S(2)}) collective-permute-start(bf16[3,128,1280]{2,1,0:T(8,128)(2,1)} %get-tuple-element.66), channel_id=1, source_target_pairs={{0,1},{1,0},{2,3},{3,2},{4,5},{5,4},{6,7},{7,6},{8,9},{9,8},{10,11... | collective-permute-start | bytes 2949128 | tf_op jit(solution)/shard_map/ppermute | solution.py:599
  13.3 2.2 copy-start.4
  15.5 0.7 copy-start.23
  16.1 3.2 %copy-start.5 = (bf16[3,128,1280]{2,1,0:T(8,128)(2,1)S(1)}, bf16[3,128,1280]{2,1,0:T(8,128)(2,1)}, u32[]{:S(2)}) copy-start(bf16[3,128,1280]{2,1,0:T(8,128)(2,1)} %get-tuple-element.65.mine.refs_0_) | copy-start | bytes 2949124
  16.1 3.6 %copy-start.22 = (s32[4]{0:T(128)S(1)}, s32[4]{0:T(128)}, u32[]{:S(2)}) copy-start(s32[4]{0:T(128)} %fusion.21.places) | copy-start | bytes 52
  29.3 3.1 %collective-permute-start.1 = (bf16[3,128,1664]{2,1,0:T(8,128)(2,1)S(1)}, bf16[3,128,1664]{2,1,0:T(8,128)(2,1)S(1)}, u32[]{:S(2)}, u32[]{:S(2)}) collective-permute-start(bf16[3,128,1664]{2,1,0:T(8,128)(2,1)S(1)} %get-tuple-element.70), channel_id=1, source_target_pairs={{0,1},{1,0},{2,3},{3,2},{4,5},{5,4},{6,7},{7,6},{8,9},{9,8},{10,11... | collective-permute-start | bytes 3833864 | tf_op jit(solution)/shard_map/ppermute | solution.py:599
  44.1 15.8 %collective-permute-start.2 = (bf16[3,128,2048]{2,1,0:T(8,128)(2,1)S(1)}, bf16[3,128,2048]{2,1,0:T(8,128)(2,1)S(1)}, u32[]{:S(2)}, u32[]{:S(2)}) collective-permute-start(bf16[3,128,2048]{2,1,0:T(8,128)(2,1)S(1)} %get-tuple-element.74), channel_id=1, source_target_pairs={{0,1},{1,0},{2,3},{3,2},{4,5},{5,4},{6,7},{7,6},{8,9},{9,8},{10,11... | collective-permute-start | bytes 4718600 | tf_op jit(solution)/shard_map/ppermute | solution.py:599
  44.3 14.8 %collective-permute-start.3 = (bf16[3,64,1280]{2,1,0:T(8,128)(2,1)S(1)}, bf16[3,64,1280]{2,1,0:T(8,128)(2,1)S(1)}, u32[]{:S(2)}, u32[]{:S(2)}) collective-permute-start(bf16[3,64,1280]{2,1,0:T(8,128)(2,1)S(1)} %get-tuple-element.75), channel_id=1, source_target_pairs={{0,2},{1,3},{2,0},{3,1},{4,6},{5,7},{6,4},{7,5},{8,10},{9,11},{10,... | collective-permute-start | bytes 1474568 | tf_op jit(solution)/shard_map/ppermute | solution.py:603
  60.0 47.6 %copy-start.14 = (bf16[2,64,1280]{2,1,0:T(8,128)(2,1)}, bf16[2,64,1280]{2,1,0:T(8,128)(2,1)S(1)}, u32[]{:S(2)}) copy-start(bf16[2,64,1280]{2,1,0:T(8,128)(2,1)S(1)} %get-tuple-element.86.refs_0_) | copy-start | bytes 983044
  69.7 18.8 %collective-permute-start.4 = (bf16[3,128,1536]{2,1,0:T(8,128)(2,1)S(1)}, bf16[3,128,1536]{2,1,0:T(8,128)(2,1)S(1)}, u32[]{:S(2)}, u32[]{:S(2)}) collective-permute-start(bf16[3,128,1536]{2,1,0:T(8,128)(2,1)S(1)} %get-tuple-element.80), channel_id=1, source_target_pairs={{0,1},{1,0},{2,3},{3,2},{4,5},{5,4},{6,7},{7,6},{8,9},{9,8},{10,11... | collective-permute-start | bytes 3538952 | tf_op jit(solution)/shard_map/ppermute | solution.py:599
  69.7 17.3 %collective-permute-start.5 = (bf16[3,64,1664]{2,1,0:T(8,128)(2,1)S(1)}, bf16[3,64,1664]{2,1,0:T(8,128)(2,1)S(1)}, u32[]{:S(2)}, u32[]{:S(2)}) collective-permute-start(bf16[3,64,1664]{2,1,0:T(8,128)(2,1)S(1)} %get-tuple-element.81), channel_id=1, source_target_pairs={{0,2},{1,3},{2,0},{3,1},{4,6},{5,7},{6,4},{7,5},{8,10},{9,11},{10,... | collective-permute-start | bytes 1916936 | tf_op jit(solution)/shard_map/ppermute | solution.py:603
  71.6 32.4 %collective-permute-start.14 = (bf16[3,64,2048]{2,1,0:T(8,128)(2,1)S(1)}, bf16[3,64,2048]{2,1,0:T(8,128)(2,1)S(1)}, u32[]{:S(2)}, u32[]{:S(2)}) collective-permute-start(bf16[3,64,2048]{2,1,0:T(8,128)(2,1)S(1)} %get-tuple-element.90), channel_id=1, source_target_pairs={{0,2},{1,3},{2,0},{3,1},{4,6},{5,7},{6,4},{7,5},{8,10},{9,11},{10,... | collective-permute-start | bytes 2359304 | tf_op jit(solution)/shard_map/ppermute | solution.py:603
  89.5 1.0 copy-start.2
  97.6 7.9 %copy-start.6 = (bf16[3,128,1024]{2,1,0:T(8,128)(2,1)}, bf16[3,128,1024]{2,1,0:T(8,128)(2,1)S(1)}, u32[]{:S(2)}) copy-start(bf16[3,128,1024]{2,1,0:T(8,128)(2,1)S(1)} %get-tuple-element.88.mine.refs_0_) | copy-start | bytes 2359300
  97.6 36.3 %collective-permute-start.13 = (bf16[3,128,1024]{2,1,0:T(8,128)(2,1)S(1)}, bf16[3,128,1024]{2,1,0:T(8,128)(2,1)S(1)}, u32[]{:S(2)}, u32[]{:S(2)}) collective-permute-start(bf16[3,128,1024]{2,1,0:T(8,128)(2,1)S(1)} %get-tuple-element.89), channel_id=1, source_target_pairs={{0,1},{1,0},{2,3},{3,2},{4,5},{5,4},{6,7},{7,6},{8,9},{9,8},{10,11... | collective-permute-start | bytes 2359304 | tf_op jit(solution)/shard_map/ppermute | solution.py:599
  97.7 13.2 %collective-permute-start.10 = (bf16[2,64,1280]{2,1,0:T(8,128)(2,1)S(1)}, bf16[2,64,1280]{2,1,0:T(8,128)(2,1)S(1)}, u32[]{:S(2)}, u32[]{:S(2)}) collective-permute-start(bf16[2,64,1280]{2,1,0:T(8,128)(2,1)S(1)} %get-tuple-element.86.refs_0_), channel_id=1, source_target_pairs={{0,2},{1,3},{2,0},{3,1},{4,6},{5,7},{6,4},{7,5},{8,10},{9,11},{10,... | collective-permute-start | bytes 983048 | tf_op jit(solution)/shard_map/ppermute | solution.py:603
  105.5 26.6 %collective-permute-start.19 = (bf16[2,64,2176]{2,1,0:T(8,128)(2,1)}, bf16[2,64,2176]{2,1,0:T(8,128)(2,1)}, u32[]{:S(2)}, u32[]{:S(2)}) collective-permute-start(bf16[2,64,2176]{2,1,0:T(8,128)(2,1)} %get-tuple-element.100.refs_0_), channel_id=1, source_target_pairs={{0,2},{1,3},{2,0},{3,1},{4,6},{5,7},{6,4},{7,5},{8,10},{9,11},{10,... | collective-permute-start | bytes 1671176 | tf_op jit(solution)/shard_map/ppermute | solution.py:603
  107.3 23.5 %collective-permute-start.7 = (bf16[2,64,1536]{2,1,0:T(8,128)(2,1)}, bf16[2,64,1536]{2,1,0:T(8,128)(2,1)}, u32[]{:S(2)}, u32[]{:S(2)}) collective-permute-start(bf16[2,64,1536]{2,1,0:T(8,128)(2,1)} %get-tuple-element.85.refs_0_), channel_id=1, source_target_pairs={{0,2},{1,3},{2,0},{3,1},{4,6},{5,7},{6,4},{7,5},{8,10},{9,11},{10,... | collective-permute-start | bytes 1179656 | tf_op jit(solution)/shard_map/ppermute | solution.py:603
  107.6 4.1 %collective-permute-start.11 = (bf16[2,64,1280]{2,1,0:T(8,128)(2,1)S(1)}, bf16[2,64,1280]{2,1,0:T(8,128)(2,1)S(1)}, u32[]{:S(2)}, u32[]{:S(2)}) collective-permute-start(bf16[2,64,1280]{2,1,0:T(8,128)(2,1)S(1)} %get-tuple-element.86.refs_0_), channel_id=1, source_target_pairs={{0,1},{1,0},{2,3},{3,2},{4,5},{5,4},{6,7},{7,6},{8,9},{9,8},{10,11... | collective-permute-start | bytes 983048 | tf_op jit(solution)/shard_map/ppermute | solution.py:599
  110.9 20.0 %collective-permute-start.12 = (bf16[2,64,1280]{2,1,0:T(8,128)(2,1)S(1)}, bf16[2,64,1280]{2,1,0:T(8,128)(2,1)S(1)}, u32[]{:S(2)}, u32[]{:S(2)}) collective-permute-start(bf16[2,64,1280]{2,1,0:T(8,128)(2,1)S(1)} %collective-permute-done.10.refs_1_), channel_id=1, source_target_pairs={{0,1},{1,0},{2,3},{3,2},{4,5},{5,4},{6,7},{7,6},{8,9},{9,8},{10,11... | collective-permute-start | bytes 983048 | tf_op jit(solution)/shard_map/ppermute | solution.py:599
  110.9 0.7 copy-start.16
  111.7 0.8 copy-start.18
  112.4 35.8 %collective-permute-start.8 = (bf16[2,64,1536]{2,1,0:T(8,128)(2,1)}, bf16[2,64,1536]{2,1,0:T(8,128)(2,1)}, u32[]{:S(2)}, u32[]{:S(2)}) collective-permute-start(bf16[2,64,1536]{2,1,0:T(8,128)(2,1)} %get-tuple-element.85.refs_0_), channel_id=1, source_target_pairs={{0,1},{1,0},{2,3},{3,2},{4,5},{5,4},{6,7},{7,6},{8,9},{9,8},{10,11... | collective-permute-start | bytes 1179656 | tf_op jit(solution)/shard_map/ppermute | solution.py:599
  130.9 18.9 %collective-permute-start.9 = (bf16[2,64,1536]{2,1,0:T(8,128)(2,1)}, bf16[2,64,1536]{2,1,0:T(8,128)(2,1)}, u32[]{:S(2)}, u32[]{:S(2)}) collective-permute-start(bf16[2,64,1536]{2,1,0:T(8,128)(2,1)} %collective-permute-done.7.refs_1_), channel_id=1, source_target_pairs={{0,1},{1,0},{2,3},{3,2},{4,5},{5,4},{6,7},{7,6},{8,9},{9,8},{10,11... | collective-permute-start | bytes 1179656 | tf_op jit(solution)/shard_map/ppermute | solution.py:599
  130.9 0.7 copy-start.20
  131.6 28.7 %collective-permute-start.20 = (bf16[2,64,2176]{2,1,0:T(8,128)(2,1)}, bf16[2,64,2176]{2,1,0:T(8,128)(2,1)}, u32[]{:S(2)}, u32[]{:S(2)}) collective-permute-start(bf16[2,64,2176]{2,1,0:T(8,128)(2,1)} %get-tuple-element.100.refs_0_), channel_id=1, source_target_pairs={{0,1},{1,0},{2,3},{3,2},{4,5},{5,4},{6,7},{7,6},{8,9},{9,8},{10,11... | collective-permute-start | bytes 1671176 | tf_op jit(solution)/shard_map/ppermute | solution.py:599
  132.2 24.8 %collective-permute-start.6 = (bf16[3,64,1536]{2,1,0:T(8,128)(2,1)}, bf16[3,64,1536]{2,1,0:T(8,128)(2,1)}, u32[]{:S(2)}, u32[]{:S(2)}) collective-permute-start(bf16[3,64,1536]{2,1,0:T(8,128)(2,1)} %get-tuple-element.84), channel_id=1, source_target_pairs={{0,2},{1,3},{2,0},{3,1},{4,6},{5,7},{6,4},{7,5},{8,10},{9,11},{10,... | collective-permute-start | bytes 1769480 | tf_op jit(solution)/shard_map/ppermute | solution.py:603
  133.9 0.9 copy-start.9
  134.8 25.6 %collective-permute-start.21 = (bf16[2,64,2176]{2,1,0:T(8,128)(2,1)}, bf16[2,64,2176]{2,1,0:T(8,128)(2,1)}, u32[]{:S(2)}, u32[]{:S(2)}) collective-permute-start(bf16[2,64,2176]{2,1,0:T(8,128)(2,1)} %collective-permute-done.19.refs_1_), channel_id=1, source_target_pairs={{0,1},{1,0},{2,3},{3,2},{4,5},{5,4},{6,7},{7,6},{8,9},{9,8},{10,11... | collective-permute-start | bytes 1671176 | tf_op jit(solution)/shard_map/ppermute | solution.py:599
  135.0 1.1 copy-start.7
  136.1 1.1 copy-start.10
  137.5 1.0 copy-start.15
  138.4 1.0 copy-start.17
  139.4 1.0 copy-start.19
  140.4 1.0 copy-start.21
  148.2 58.1 %collective-permute-start.36 = (bf16[256,2048]{1,0:T(8,128)(2,1)S(1)}, bf16[256,2048]{1,0:T(8,128)(2,1)}, u32[]{:S(2)}, u32[]{:S(2)}) collective-permute-start(bf16[256,2048]{1,0:T(8,128)(2,1)S(1)} %copy-done.1), channel_id=1, source_target_pairs={{0,16},{16,0},{1,17},{17,1},{2,18},{18,2},{3,19},{19,3},{4,20},{20... | collective-permute-start | bytes 3145736 | tf_op jit(solution)/shard_map/ppermute | solution.py:606
  149.8 19.4 %collective-permute-start.18 = (bf16[3,64,1024]{2,1,0:T(8,128)(2,1)S(1)}, bf16[3,64,1024]{2,1,0:T(8,128)(2,1)S(1)}, u32[]{:S(2)}, u32[]{:S(2)}) collective-permute-start(bf16[3,64,1024]{2,1,0:T(8,128)(2,1)S(1)} %get-tuple-element.99), channel_id=1, source_target_pairs={{0,2},{1,3},{2,0},{3,1},{4,6},{5,7},{6,4},{7,5},{8,10},{9,11},{10,... | collective-permute-start | bytes 1179656 | tf_op jit(solution)/shard_map/ppermute | solution.py:603
  150.1 6.9 %copy-start.3 = (bf16[3,128,1536]{2,1,0:T(8,128)(2,1)S(1)}, bf16[3,128,1536]{2,1,0:T(8,128)(2,1)}, u32[]{:S(2)}) copy-start(bf16[3,128,1536]{2,1,0:T(8,128)(2,1)} %copy-done.2) | copy-start | bytes 3538948
  158.5 18.4 %collective-permute-start.15 = (bf16[2,64,1536]{2,1,0:T(8,128)(2,1)S(1)}, bf16[2,64,1536]{2,1,0:T(8,128)(2,1)S(1)}, u32[]{:S(2)}, u32[]{:S(2)}) collective-permute-start(bf16[2,64,1536]{2,1,0:T(8,128)(2,1)S(1)} %get-tuple-element.98.refs_1_), channel_id=1, source_target_pairs={{0,2},{1,3},{2,0},{3,1},{4,6},{5,7},{6,4},{7,5},{8,10},{9,11},{10,... | collective-permute-start | bytes 1179656 | tf_op jit(solution)/shard_map/ppermute | solution.py:603
  160.3 8.9 %copy-start.8 = (bf16[3,128,1024]{2,1,0:T(8,128)(2,1)S(1)}, bf16[3,128,1024]{2,1,0:T(8,128)(2,1)}, u32[]{:S(2)}) copy-start(bf16[3,128,1024]{2,1,0:T(8,128)(2,1)} %copy-done.6) | copy-start | bytes 2359300
  160.3 8.9 %copy-start.11 = (bf16[3,128,1024]{2,1,0:T(8,128)(2,1)S(1)}, bf16[3,128,1024]{2,1,0:T(8,128)(2,1)}, u32[]{:S(2)}) copy-start(bf16[3,128,1024]{2,1,0:T(8,128)(2,1)} %copy-done.9) | copy-start | bytes 2359300
  169.2 11.6 %copy-start.13 = (bf16[2048,64]{0,1:T(8,128)(2,1)S(1)}, bf16[2048,64]{0,1:T(8,128)(2,1)}, u32[]{:S(2)}) copy-start(bf16[2048,64]{0,1:T(8,128)(2,1)} %param.13) | copy-start | bytes 786436
  171.2 6.8 %collective-permute-start.25 = (bf16[256,64]{1,0:T(8,128)(2,1)S(1)}, bf16[256,64]{1,0:T(8,128)(2,1)S(1)}, u32[]{:S(2)}, u32[]{:S(2)}) collective-permute-start(bf16[256,64]{1,0:T(8,128)(2,1)S(1)} %get-tuple-element.110), channel_id=1, source_target_pairs={{0,4},{4,8},{8,12},{12,0},{1,5},{5,9},{9,13},{13,1},{2,6},{6,10},{... | collective-permute-start | bytes 98312 | tf_op jit(solution)/shard_map/ppermute | solution.py:606
  172.9 7.4 %collective-permute-start.26 = (bf16[256,64]{1,0:T(8,128)(2,1)S(1)}, bf16[256,64]{1,0:T(8,128)(2,1)S(1)}, u32[]{:S(2)}, u32[]{:S(2)}) collective-permute-start(bf16[256,64]{1,0:T(8,128)(2,1)S(1)} %get-tuple-element.110), channel_id=1, source_target_pairs={{0,8},{4,12},{8,0},{12,4},{1,9},{5,13},{9,1},{13,5},{2,10},{6,14},... | collective-permute-start | bytes 98312 | tf_op jit(solution)/shard_map/ppermute | solution.py:606
  175.5 4.8 %collective-permute-start.27 = (bf16[256,64]{1,0:T(8,128)(2,1)S(1)}, bf16[256,64]{1,0:T(8,128)(2,1)S(1)}, u32[]{:S(2)}, u32[]{:S(2)}) collective-permute-start(bf16[256,64]{1,0:T(8,128)(2,1)S(1)} %get-tuple-element.110), channel_id=1, source_target_pairs={{0,12},{4,0},{8,4},{12,8},{1,13},{5,1},{9,5},{13,9},{2,14},{6,2},{... | collective-permute-start | bytes 98312 | tf_op jit(solution)/shard_map/ppermute | solution.py:606
  176.9 9.1 %collective-permute-start.16 = (bf16[2,64,1536]{2,1,0:T(8,128)(2,1)S(1)}, bf16[2,64,1536]{2,1,0:T(8,128)(2,1)S(1)}, u32[]{:S(2)}, u32[]{:S(2)}) collective-permute-start(bf16[2,64,1536]{2,1,0:T(8,128)(2,1)S(1)} %get-tuple-element.98.refs_1_), channel_id=1, source_target_pairs={{0,1},{1,0},{2,3},{3,2},{4,5},{5,4},{6,7},{7,6},{8,9},{9,8},{10,11... | collective-permute-start | bytes 1179656 | tf_op jit(solution)/shard_map/ppermute | solution.py:599
  178.0 7.7 %collective-permute-start.22 = (bf16[2,64,1024]{2,1,0:T(8,128)(2,1)S(1)}, bf16[2,64,1024]{2,1,0:T(8,128)(2,1)S(1)}, u32[]{:S(2)}, u32[]{:S(2)}) collective-permute-start(bf16[2,64,1024]{2,1,0:T(8,128)(2,1)S(1)} %get-tuple-element.104.refs_5_), channel_id=1, source_target_pairs={{0,2},{1,3},{2,0},{3,1},{4,6},{5,7},{6,4},{7,5},{8,10},{9,11},{10,... | collective-permute-start | bytes 786440 | tf_op jit(solution)/shard_map/ppermute | solution.py:603
  180.3 6.4 %collective-permute-start.23 = (bf16[2,64,1024]{2,1,0:T(8,128)(2,1)S(1)}, bf16[2,64,1024]{2,1,0:T(8,128)(2,1)S(1)}, u32[]{:S(2)}, u32[]{:S(2)}) collective-permute-start(bf16[2,64,1024]{2,1,0:T(8,128)(2,1)S(1)} %get-tuple-element.104.refs_5_), channel_id=1, source_target_pairs={{0,1},{1,0},{2,3},{3,2},{4,5},{5,4},{6,7},{7,6},{8,9},{9,8},{10,11... | collective-permute-start | bytes 786440 | tf_op jit(solution)/shard_map/ppermute | solution.py:599
  180.3 7.9 %collective-permute-start.17 = (bf16[2,64,1536]{2,1,0:T(8,128)(2,1)S(1)}, bf16[2,64,1536]{2,1,0:T(8,128)(2,1)S(1)}, u32[]{:S(2)}, u32[]{:S(2)}) collective-permute-start(bf16[2,64,1536]{2,1,0:T(8,128)(2,1)S(1)} %collective-permute-done.15.refs_2_), channel_id=1, source_target_pairs={{0,1},{1,0},{2,3},{3,2},{4,5},{5,4},{6,7},{7,6},{8,9},{9,8},{10,11... | collective-permute-start | bytes 1179656 | tf_op jit(solution)/shard_map/ppermute | solution.py:599
  185.7 2.4 %collective-permute-start.24 = (bf16[2,64,1024]{2,1,0:T(8,128)(2,1)S(1)}, bf16[2,64,1024]{2,1,0:T(8,128)(2,1)S(1)}, u32[]{:S(2)}, u32[]{:S(2)}) collective-permute-start(bf16[2,64,1024]{2,1,0:T(8,128)(2,1)S(1)} %collective-permute-done.22.refs_6_), channel_id=1, source_target_pairs={{0,1},{1,0},{2,3},{3,2},{4,5},{5,4},{6,7},{7,6},{8,9},{9,8},{10,11... | collective-permute-start | bytes 786440 | tf_op jit(solution)/shard_map/ppermute | solution.py:599
  186.0 17.8 %collective-permute-start.35 = (bf16[256,65]{1,0:T(8,128)(2,1)S(1)}, bf16[256,65]{1,0:T(8,128)(2,1)S(1)}, u32[]{:S(2)}, u32[]{:S(2)}) collective-permute-start(bf16[256,65]{1,0:T(8,128)(2,1)S(1)} %pad_maximum_fusion.1), channel_id=1, source_target_pairs={{0,16},{16,0},{1,17},{17,1},{2,18},{18,2},{3,19},{19,3},{4,20},{20... | collective-permute-start | bytes 99848 | tf_op jit(solution)/shard_map/ppermute | solution.py:606
  186.6 30.4 %collective-permute-start.34 = (f32[64,2048]{1,0:T(8,128)S(1)}, f32[64,2048]{1,0:T(8,128)}, u32[]{:S(2)}, u32[]{:S(2)}) collective-permute-start(f32[64,2048]{1,0:T(8,128)S(1)} %fusion.33), channel_id=1, source_target_pairs={{0,16},{16,0},{1,17},{17,1},{2,18},{18,2},{3,19},{19,3},{4,20},{20... | collective-permute-start | bytes 1572872 | tf_op jit(solution)/shard_map/ppermute | solution.py:606
  204.9 13.7 %collective-permute-start.31 = (bf16[64,1024]{1,0:T(8,128)(2,1)S(1)}, bf16[64,1024]{1,0:T(8,128)(2,1)S(1)}, u32[]{:S(2)}, u32[]{:S(2)}) collective-permute-start(bf16[64,1024]{1,0:T(8,128)(2,1)S(1)} %get-tuple-element.116), channel_id=1, source_target_pairs={{0,4},{4,8},{8,12},{12,0},{1,5},{5,9},{9,13},{13,1},{2,6},{6,10},{... | collective-permute-start | bytes 393224 | tf_op jit(solution)/shard_map/ppermute | solution.py:606
  205.6 17.8 %collective-permute-start.32 = (bf16[64,1024]{1,0:T(8,128)(2,1)S(1)}, bf16[64,1024]{1,0:T(8,128)(2,1)S(1)}, u32[]{:S(2)}, u32[]{:S(2)}) collective-permute-start(bf16[64,1024]{1,0:T(8,128)(2,1)S(1)} %get-tuple-element.117), channel_id=1, source_target_pairs={{0,8},{4,12},{8,0},{12,4},{1,9},{5,13},{9,1},{13,5},{2,10},{6,14},... | collective-permute-start | bytes 393224 | tf_op jit(solution)/shard_map/ppermute | solution.py:606
  206.3 24.8 %copy-start.24 = (f32[64,2048]{1,0:T(8,128)S(1)}, f32[64,2048]{1,0:T(8,128)}, u32[]{:S(2)}) copy-start(f32[64,2048]{1,0:T(8,128)} %fusion.15) | copy-start | bytes 1572868
  213.7 9.7 %collective-permute-start.33 = (bf16[64,1024]{1,0:T(8,128)(2,1)S(1)}, bf16[64,1024]{1,0:T(8,128)(2,1)S(1)}, u32[]{:S(2)}, u32[]{:S(2)}) collective-permute-start(bf16[64,1024]{1,0:T(8,128)(2,1)S(1)} %get-tuple-element.118), channel_id=1, source_target_pairs={{0,12},{4,0},{8,4},{12,8},{1,13},{5,1},{9,5},{13,9},{2,14},{6,2},{... | collective-permute-start | bytes 393224 | tf_op jit(solution)/shard_map/ppermute | solution.py:606
  216.5 8.3 %collective-permute-start.28 = (bf16[64,1024]{1,0:T(8,128)(2,1)S(1)}, bf16[64,1024]{1,0:T(8,128)(2,1)S(1)}, u32[]{:S(2)}, u32[]{:S(2)}) collective-permute-start(bf16[64,1024]{1,0:T(8,128)(2,1)S(1)} %get-tuple-element.111), channel_id=1, source_target_pairs={{0,4},{4,8},{8,12},{12,0},{1,5},{5,9},{9,13},{13,1},{2,6},{6,10},{... | collective-permute-start | bytes 393224 | tf_op jit(solution)/shard_map/ppermute | solution.py:606
  217.1 14.1 %collective-permute-start.29 = (bf16[64,1024]{1,0:T(8,128)(2,1)S(1)}, bf16[64,1024]{1,0:T(8,128)(2,1)S(1)}, u32[]{:S(2)}, u32[]{:S(2)}) collective-permute-start(bf16[64,1024]{1,0:T(8,128)(2,1)S(1)} %get-tuple-element.112), channel_id=1, source_target_pairs={{0,8},{4,12},{8,0},{12,4},{1,9},{5,13},{9,1},{13,5},{2,10},{6,14},... | collective-permute-start | bytes 393224 | tf_op jit(solution)/shard_map/ppermute | solution.py:606
  218.5 12.6 %collective-permute-start.30 = (bf16[64,1024]{1,0:T(8,128)(2,1)S(1)}, bf16[64,1024]{1,0:T(8,128)(2,1)S(1)}, u32[]{:S(2)}, u32[]{:S(2)}) collective-permute-start(bf16[64,1024]{1,0:T(8,128)(2,1)S(1)} %get-tuple-element.113), channel_id=1, source_target_pairs={{0,12},{4,0},{8,4},{12,8},{1,13},{5,1},{9,5},{13,9},{2,14},{6,2},{... | collective-permute-start | bytes 393224 | tf_op jit(solution)/shard_map/ppermute | solution.py:606
